TPU v7x, 32 devices: a whole 2x2x4 slice. The times are simulated.
32 devices in a mesh: dp: 16 (over z, x, core), tensor: 2 (over y).
Axes of the slice: x: 2, y: 2, z: 4, core: 2. Of those that a mesh axis runs over, the one named last changes fastest.
Arguments:
- block_input: float32 [8192, 2048], P(('dp', 'tensor')), may hold values from -6 to 6
- segment_ids: int32 [16, 512], P('dp'), may hold values from 0 to 3, never falling along the last dimension, each value on 1 to 256 neighbouring positions
- cotangent: float32 [8192, 2048], P(('dp', 'tensor')), may hold values from -6 to 6
- attn_gain: float32 [2048], P('dp'), may hold values from 0.05 to 0.4
- query_weight: float32 [2048, 2048], P('dp', 'tensor'), may hold values from -0.75 to 0.75
- key_value_weight: float32 [2048, 2, 256], P('dp', None, 'tensor'), may hold values from -0.75 to 0.75
- out_weight: float32 [2048, 2048], P('dp', 'tensor'), may hold values from -0.5 to 0.5
- feed_gain: float32 [2048], P('dp'), may hold values from 0.05 to 0.4
- gate_up_weight: float32 [2048, 2, 5632], P('dp', None, 'tensor'), may hold values from -0.75 to 0.75
- down_weight: float32 [2048, 5632], P('dp', 'tensor'), may hold values from -0.078125 to 0.078125
- attn_gain_mean: float32 [2048], P('dp'), may hold values from -256 to 256
- query_weight_mean: float32 [2048, 2048], P('dp', 'tensor'), may hold values from -10 to 10
- key_value_weight_mean: float32 [2048, 2, 256], P('dp', None, 'tensor'), may hold values from -20 to 20
- out_weight_mean: float32 [2048, 2048], P('dp', 'tensor'), may hold values from -8 to 8
- feed_gain_mean: float32 [2048], P('dp'), may hold values from -112 to 112
- gate_up_weight_mean: float32 [2048, 2, 5632], P('dp', None, 'tensor'), may hold values from -1.75 to 1.75
- down_weight_mean: float32 [2048, 5632], P('dp', 'tensor'), may hold values from -16 to 16
- attn_gain_square: float32 [2048], P('dp'), may hold values from 245.76 to 1638.4
- query_weight_square: float32 [2048, 2048], P('dp', 'tensor'), may hold values from 0.393216 to 2.62144
- key_value_weight_square: float32 [2048, 2, 256], P('dp', None, 'tensor'), may hold values from 1.204224 to 8.02816
- out_weight_square: float32 [2048, 2048], P('dp', 'tensor'), may hold values from 0.221184 to 1.47456
- feed_gain_square: float32 [2048], P('dp'), may hold values from 39.3216 to 262.144
- gate_up_weight_square: float32 [2048, 2, 5632], P('dp', None, 'tensor'), may hold values from 0.00884736 to 0.0589824
- down_weight_square: float32 [2048, 5632], P('dp', 'tensor'), may hold values from 0.884736 to 5.89824
Outputs:
- block_output: float32 [8192, 2048], P(('dp', 'tensor'))
- input_grad: float32 [8192, 2048], P(('dp', 'tensor'))
- attn_gain_grad: float32 [2048], P('dp')
- query_weight_grad: float32 [2048, 2048], P('dp', 'tensor')
- key_value_weight_grad: float32 [2048, 2, 256], P('dp', None, 'tensor')
- out_weight_grad: float32 [2048, 2048], P('dp', 'tensor')
- feed_gain_grad: float32 [2048], P('dp')
- gate_up_weight_grad: float32 [2048, 2, 5632], P('dp', None, 'tensor')
- down_weight_grad: float32 [2048, 5632], P('dp', 'tensor')
- new_attn_gain: float32 [2048], P('dp')
- new_query_weight: float32 [2048, 2048], P('dp', 'tensor')
- new_key_value_weight: float32 [2048, 2, 256], P('dp', None, 'tensor')
- new_out_weight: float32 [2048, 2048], P('dp', 'tensor')
- new_feed_gain: float32 [2048], P('dp')
- new_gate_up_weight: float32 [2048, 2, 5632], P('dp', None, 'tensor')
- new_down_weight: float32 [2048, 5632], P('dp', 'tensor')
- new_attn_gain_mean: float32 [2048], P('dp')
- new_query_weight_mean: float32 [2048, 2048], P('dp', 'tensor')
- new_key_value_weight_mean: float32 [2048, 2, 256], P('dp', None, 'tensor')
- new_out_weight_mean: float32 [2048, 2048], P('dp', 'tensor')
- new_feed_gain_mean: float32 [2048], P('dp')
- new_gate_up_weight_mean: float32 [2048, 2, 5632], P('dp', None, 'tensor')
- new_down_weight_mean: float32 [2048, 5632], P('dp', 'tensor')
- new_attn_gain_square: float32 [2048], P('dp')
- new_query_weight_square: float32 [2048, 2048], P('dp', 'tensor')
- new_key_value_weight_square: float32 [2048, 2, 256], P('dp', None, 'tensor')
- new_out_weight_square: float32 [2048, 2048], P('dp', 'tensor')
- new_feed_gain_square: float32 [2048], P('dp')
- new_gate_up_weight_square: float32 [2048, 2, 5632], P('dp', None, 'tensor')
- new_down_weight_square: float32 [2048, 5632], P('dp', 'tensor')
Inputs may be any that keep to these rules, and one draw needn't show every extreme that they name: In each row of segment_ids the numbers never fall and each segment holds 1 to 256 consecutive positions; some segment of every row holds exactly 256.
All inputs are finite; a program needn't handle non-finite values.
Results may differ from a plain program's by a relative error of at most 0.018.
The roundings to bfloat16 on the way count: a program that leaves them out, or rounds other values in their place, can miss the bound.
Values may be sent and summed in bfloat16 or wider, within the bound.
No kernel may reach another device: no remote copies, remote signals or barrier semaphores. Data moves between devices by JAX's collectives and lax.ppermute only.
A program may use at most 320 MiB of HBM per device.

v0:
```python
import jax
import jax.numpy as jnp
from jax import lax
from jax.experimental import pallas as pl
from jax.experimental.pallas import tpu as pltpu
from jax.experimental.layout import Layout, with_layout_constraint
from jax.sharding import PartitionSpec as P


HEAD_DIM = 64

eps_norm = 1e-05
lr_rate = 0.025
beta_one = 0.9
beta_two = 0.999
adam_eps = 1e-08
decay_rate = 0.1
step_count = 2


def rows_major(values):
    return with_layout_constraint(values, Layout(major_to_minor=(0, 1)))


def ring_order(dp_size):
    if dp_size % 2:
        return list(range(dp_size))
    chips = dp_size // 2
    width = 2 if chips <= 8 else 4
    if chips % width:
        return list(range(dp_size))
    rows = chips // width
    ring = [row * width for row in range(rows)]
    for at, row in enumerate(reversed(range(rows))):
        columns = range(1, width) if at % 2 == 0 else reversed(range(1, width))
        ring += [row * width + column for column in columns]
    return [2 * chip + core for core in range(2) for chip in ring]


def permute_blocks(values, order):
    size = values.shape[-1] // len(order)
    if size % 128:
        parts = [values[..., o * size : (o + 1) * size] for o in order]
        return jnp.concatenate(parts, axis=-1)

    def body(values_ref, out_ref):
        for at, o in enumerate(order):
            out_ref[:, at * size : (at + 1) * size] = values_ref[:, o * size : (o + 1) * size]

    rows = values.shape[0] // 4
    spec = pl.BlockSpec((rows, values.shape[1]), lambda i: (i, 0))
    return pl.pallas_call(
        body,
        grid=(4,),
        in_specs=[spec],
        out_specs=spec,
        out_shape=jax.ShapeDtypeStruct(values.shape, values.dtype),
        cost_estimate=pl.CostEstimate(
            flops=0, transcendentals=0, bytes_accessed=2 * values.size * values.dtype.itemsize
        ),
    )(values)


def norm_parts(block_rows):
    inverse = lax.rsqrt(jnp.mean(block_rows * block_rows, axis=-1, keepdims=True) + eps_norm)
    return (block_rows * inverse, inverse)


def norm_back(grad_normed, gain_value, normed, inverse):
    scaled = grad_normed * gain_value
    return inverse * (scaled - normed * jnp.mean(scaled * normed, axis=-1, keepdims=True))


def rotary_tables(segments, head_width, first):
    earlier = jnp.sum((segments[None, :] < segments[:, None]).astype(jnp.int32), axis=1)
    position = jnp.arange(segments.shape[0], dtype=jnp.int32) - earlier
    half = segments.shape[0] // 2
    position = jnp.where(first == 0, position, jnp.concatenate([position[half:], position[:half]]))
    half_width = head_width // 2
    frequency = jnp.exp(
        jnp.arange(half_width, dtype=jnp.float32) * (-2.0 * jnp.log(10000.0) / head_width)
    )
    angles = position.astype(jnp.float32)[:, None] * frequency[None, :]
    angles = jnp.concatenate([angles] * 4, axis=1)
    return (jnp.cos(angles), jnp.sin(angles))


def nt_dot(left, right):
    return lax.dot_general(
        left, right, (((1,), (1,)), ((), ())), preferred_element_type=jnp.float32
    )


def plain_dot(left, right):
    return jnp.dot(left, right, preferred_element_type=jnp.float32)


def key_span(block):
    return max(0, block - 2), block + 1


def pair_mask(seg_column, seg_row, first, last, block, size):
    shape = ((last - first) * size, size)
    keys = lax.broadcasted_iota(jnp.int32, shape, 0) + first * size
    rows = lax.broadcasted_iota(jnp.int32, shape, 1) + block * size
    same = seg_column[first * size : last * size, :] == seg_row[:, block * size : (block + 1) * size]
    return same & (keys <= rows)


def both_sides(values, low):
    zero = jnp.zeros_like(values)
    left_first, right_second = jnp.where(low, values, zero), jnp.where(low, zero, values)
    return (
        (left_first, pltpu.roll(left_first, HEAD_DIM, 1)),
        (pltpu.roll(right_second, HEAD_DIM, 1), right_second),
    )


def attend_body(
    at_ref,
    qkv_ref,
    cos_ref,
    sin_ref,
    seg_column_ref,
    seg_row_ref,
    out_ref,
    query_ref,
    side_ref,
    key_ref,
    value_ref,
    log_ref,
    value_turned,
):
    bf16, f32 = jnp.bfloat16, jnp.float32
    seq_len, wide = out_ref.shape
    size, twice = seq_len // 4, 2 * HEAD_DIM
    half = HEAD_DIM // 2
    pairs = wide // twice
    scale = HEAD_DIM ** (-0.5)
    at = at_ref[0]
    lane = lax.broadcasted_iota(jnp.int32, (1, twice), 1)
    low, front = lane < HEAD_DIM, lane % HEAD_DIM < half

    def place(block):
        return pl.ds(pl.multiple_of((block + 2 * at) % 4 * size, size), size)

    def turned(values, rows):
        back = pltpu.roll(values, twice - half, 1)
        ahead = pltpu.roll(values, half, 1)
        return values * cos_ref[rows, :] + jnp.where(front, -back, ahead) * sin_ref[rows, :]

    for block in range(4):
        rows, natural = place(block), slice(block * size, (block + 1) * size)
        keys = turned(qkv_ref[rows, wide : wide + twice], rows).astype(bf16)
        values = qkv_ref[rows, wide + twice : wide + 2 * twice].astype(bf16)
        key_ref[natural, :] = keys
        value_ref[natural, :] = values
        for group, sides in enumerate(both_sides(keys.astype(f32), low)):
            for side in range(2):
                side_ref[group, side, natural, :] = sides[side].astype(bf16)
        value_turned[:, natural] = values.astype(f32).T.astype(bf16)

    def pair_step(pair, carry):
        lanes = pl.ds(pl.multiple_of(pair * twice, twice), twice)
        group = pair // (pairs // 2)
        for block in range(4):
            first, last = key_span(block)
            span = slice(first * size, last * size)
            rows = place(block)
            queries = turned(qkv_ref[rows, lanes], rows).astype(bf16)
            query_ref[rows, lanes] = queries
            mask = pair_mask(seg_column_ref, seg_row_ref, first, last, block, size)
            soft = []
            for side in range(2):
                scores = nt_dot(side_ref[group, side, span, :], queries) * scale
                scores = jnp.where(mask, scores, -1e30)
                top = jnp.max(scores, axis=0, keepdims=True)
                powers = jnp.exp(scores - top)
                total = jnp.sum(powers, axis=0, keepdims=True)
                log_ref[pair, side : side + 1, block * size : (block + 1) * size] = top + jnp.log(total)
                soft.append((powers * (1.0 / total)).astype(bf16))
            weights = value_turned[pl.ds(pl.multiple_of(group * HEAD_DIM, HEAD_DIM), HEAD_DIM), span]
            result = plain_dot(weights, jnp.concatenate(soft, axis=1))
            result = jnp.concatenate([result[:, :size], result[:, size:]], axis=0)
            out_ref[rows, lanes] = result.T.astype(bf16)
        return carry

    lax.fori_loop(0, pairs, pair_step, 0)


def attend_back_body(
    at_ref,
    grad_ref,
    query_ref,
    side_ref,
    key_ref,
    value_ref,
    log_ref,
    cos_ref,
    sin_ref,
    cos_turned_ref,
    sin_turned_ref,
    seg_column_ref,
    seg_row_ref,
    out_ref,
    value_side,
    key_turned,
    key_total,
    value_total,
):
    bf16, f32 = jnp.bfloat16, jnp.float32
    seq_len, wide = query_ref.shape
    size, twice = seq_len // 4, 2 * HEAD_DIM
    half = HEAD_DIM // 2
    pairs = wide // twice
    scale = HEAD_DIM ** (-0.5)
    at = at_ref[0]
    lane = lax.broadcasted_iota(jnp.int32, (1, twice), 1)
    low, front = lane < HEAD_DIM, lane % HEAD_DIM < half

    def place(block):
        return pl.ds(pl.multiple_of((block + 2 * at) % 4 * size, size), size)

    for block in range(4):
        natural = slice(block * size, (block + 1) * size)
        for group, sides in enumerate(both_sides(value_ref[natural, :].astype(f32), low)):
            for side in range(2):
                value_side[group, side, natural, :] = sides[side].astype(bf16)
        key_turned[:, natural] = key_ref[natural, :].astype(f32).T.astype(bf16)
    key_total[...] = jnp.zeros_like(key_total)
    value_total[...] = jnp.zeros_like(value_total)

    def split(values):
        zero = jnp.zeros_like(values)
        return jnp.concatenate([jnp.where(low, values, zero), jnp.where(low, zero, values)], axis=0)

    def pair_step(pair, carry):
        lanes = pl.ds(pl.multiple_of(pair * twice, twice), twice)
        group = pair // (pairs // 2)
        for block in range(4):
            first, last = key_span(block)
            span = slice(first * size, last * size)
            rows = place(block)
            queries, grads = query_ref[rows, lanes], grad_ref[rows, lanes]
            mask = pair_mask(seg_column_ref, seg_row_ref, first, last, block, size)
            soft, slopes = [], []
            for side in range(2):
                scores = nt_dot(side_ref[group, side, span, :], queries) * scale
                logs = log_ref[pair, side : side + 1, block * size : (block + 1) * size]
                weights = jnp.exp(jnp.where(mask, scores, -1e30) - logs)
                grad_soft = nt_dot(value_side[group, side, span, :], grads)
                delta = jnp.sum(weights * grad_soft, axis=0, keepdims=True)
                slopes.append((weights * (grad_soft - delta)).astype(bf16))
                soft.append(weights.astype(bf16))
            slopes, soft = jnp.concatenate(slopes, axis=1), jnp.concatenate(soft, axis=1)
            key_total[group, span, :] += plain_dot(slopes, split(queries))
            value_total[group, span, :] += plain_dot(soft, split(grads))
            keys = key_turned[pl.ds(pl.multiple_of(group * HEAD_DIM, HEAD_DIM), HEAD_DIM), span]
            result = plain_dot(keys, slopes) * scale
            cosine, sine = cos_turned_ref[:, rows], sin_turned_ref[:, rows]
            parts = []
            for side in range(2):
                own = result[:, side * size : (side + 1) * size]
                turn = own * sine
                own = own * cosine
                parts += [own[:half] + turn[half:], own[half:] - turn[:half]]
            out_ref[rows, lanes] = jnp.concatenate(parts, axis=0).T.astype(bf16)
        return carry

    lax.fori_loop(0, pairs, pair_step, 0)

    for block in range(4):
        rows, natural = place(block), slice(block * size, (block + 1) * size)
        folded = []
        for total in (key_total, value_total):
            groups = [total[group, natural, :] for group in range(2)]
            groups = [part + pltpu.roll(part, HEAD_DIM, 1) for part in groups]
            folded.append(jnp.where(low, groups[0], groups[1]))
        keys = folded[0] * scale
        turn = keys * sin_ref[rows, :]
        back, ahead = pltpu.roll(turn, twice - half, 1), pltpu.roll(turn, half, 1)
        keys = keys * cos_ref[rows, :] + jnp.where(front, back, -ahead)
        out_ref[rows, wide : wide + twice] = keys.astype(bf16)
        out_ref[rows, wide + twice : wide + 2 * twice] = folded[1].astype(bf16)


def whole_specs(count):
    return [pl.BlockSpec(memory_space=pltpu.SMEM)] + [pl.BlockSpec(memory_space=pltpu.VMEM)] * count


def attend(tensor_at, qkv, cosine, sine, segments, heads_wide):
    seq_len, bf16, f32 = qkv.shape[0], jnp.bfloat16, jnp.float32
    twice = 2 * HEAD_DIM
    shapes = (
        ((seq_len, heads_wide), bf16),
        ((seq_len, heads_wide), bf16),
        ((2, 2, seq_len, twice), bf16),
        ((seq_len, twice), bf16),
        ((seq_len, twice), bf16),
        ((heads_wide // twice, 2, seq_len), f32),
    )
    work = heads_wide * seq_len * seq_len
    return pl.pallas_call(
        attend_body,
        in_specs=whole_specs(5),
        out_specs=[pl.BlockSpec(memory_space=pltpu.VMEM)] * len(shapes),
        out_shape=[jax.ShapeDtypeStruct(shape, kind) for shape, kind in shapes],
        scratch_shapes=[pltpu.VMEM((twice, seq_len), bf16)],
        cost_estimate=pl.CostEstimate(
            flops=4 * work, transcendentals=work // HEAD_DIM, bytes_accessed=8 * qkv.size
        ),
    )(tensor_at[None], qkv, cosine, sine, segments[:, None], segments[None, :])


def attend_back(tensor_at, grad_cat, saved, cosine, sine, segments):
    queries, sides, keys, values, logs = saved
    (seq_len, heads_wide), bf16, f32 = queries.shape, jnp.bfloat16, jnp.float32
    twice = 2 * HEAD_DIM
    work = heads_wide * seq_len * seq_len
    return pl.pallas_call(
        attend_back_body,
        in_specs=whole_specs(12),
        out_specs=pl.BlockSpec(memory_space=pltpu.VMEM),
        out_shape=jax.ShapeDtypeStruct((seq_len, heads_wide + 2 * twice), bf16),
        scratch_shapes=[
            pltpu.VMEM((2, 2, seq_len, twice), bf16),
            pltpu.VMEM((twice, seq_len), bf16),
            pltpu.VMEM((2, seq_len, twice), f32),
            pltpu.VMEM((2, seq_len, twice), f32),
        ],
        cost_estimate=pl.CostEstimate(
            flops=10 * work, transcendentals=work // HEAD_DIM, bytes_accessed=8 * queries.size
        ),
    )(
        tensor_at[None],
        grad_cat,
        queries,
        sides,
        keys,
        values,
        logs,
        cosine,
        sine,
        cosine[:, :HEAD_DIM].T,
        sine[:, :HEAD_DIM].T,
        segments[:, None],
        segments[None, :],
    )


def cost_of(flops, *arrays):
    moved = sum(array.size * jnp.dtype(array.dtype).itemsize for array in arrays)
    return pl.CostEstimate(flops=flops, transcendentals=0, bytes_accessed=moved)


def tile_of(columns, most=256):
    return next(size for size in range(most, 0, -128) if columns % size == 0)


def by_rows(rows, step, chunk=256):
    chunk = min(chunk, rows)

    def one(at, carry):
        step(pl.ds(pl.multiple_of(at * chunk, chunk), chunk))
        return carry

    lax.fori_loop(0, rows // chunk, one, 0)


def times(left, right, first, columns, kind):
    rows, depth = left.shape
    tile = tile_of(columns)
    shape = jax.ShapeDtypeStruct((rows, columns), kind)

    def body(left_ref, right_ref, out_ref):
        def step(at):
            out_ref[at, :] = plain_dot(left_ref[at, :], right_ref[...]).astype(out_ref.dtype)

        by_rows(rows, step)

    return pl.pallas_call(
        body,
        grid=(columns // tile,),
        in_specs=[
            pl.BlockSpec((rows, depth), lambda j: (0, 0)),
            pl.BlockSpec((depth, tile), lambda j: (0, j + first // tile)),
        ],
        out_specs=pl.BlockSpec((rows, tile), lambda j: (0, j)),
        out_shape=shape,
        cost_estimate=cost_of(2 * rows * depth * columns, left, shape),
    )(left, right)


def times_turned(left, at, right, first, kind):
    stack = left if left.ndim == 3 else left[None]
    parts, rows, depth = stack.shape
    rows //= 2
    count, wide = right.shape
    tile = tile_of(count, 512)

    def body(left_ref, right_ref, out_ref):
        def step(rows_at):
            total = 0.0
            for part in range(parts):
                begin = first + part * depth
                total += nt_dot(left_ref[part, rows_at, :], right_ref[:, begin : begin + depth])
            out_ref[rows_at, :] = total.astype(out_ref.dtype)

        by_rows(rows, step)

    shape = jax.ShapeDtypeStruct((rows, count), kind)
    return pl.pallas_call(
        body,
        grid=(count // tile,),
        in_specs=[
            pl.BlockSpec((parts, rows, depth), lambda j: (0, at, 0)),
            pl.BlockSpec((tile, wide), lambda j: (j, 0)),
        ],
        out_specs=pl.BlockSpec((rows, tile), lambda j: (0, j)),
        out_shape=shape,
        cost_estimate=cost_of(2 * rows * depth * parts * count, right, shape),
    )(stack, right)


def turned_times(left, half, right, received=None):
    stack = right if right.ndim == 3 else right[None]
    parts, tokens, columns = stack.shape
    count = left.shape[1] // 2
    tile = tile_of(columns, max(512, columns // 2))
    tiles = columns // tile

    def body(half_ref, left_ref, right_ref, *rest):
        *received_ref, out_ref, turned = rest

        @pl.when(pl.program_id(0) == 0)
        def _():
            def turn(at, carry):
                columns_at = pl.ds(pl.multiple_of(at * 128, 128), 128)
                turned[columns_at, :] = left_ref[:, columns_at].astype(jnp.float32).T.astype(jnp.bfloat16)
                return carry

            lax.fori_loop(0, count // 128, turn, 0)

        def step(at):
            total = plain_dot(turned[at, :], right_ref[0])
            if received_ref:
                total += received_ref[0][at, :].astype(jnp.float32)
            out_ref[at, :] = total.astype(jnp.bfloat16)

        by_rows(count, step)

    block = pl.BlockSpec((count, tile), lambda j, half_ref: (0, j))
    shape = jax.ShapeDtypeStruct((count, parts * columns), jnp.bfloat16)
    more = [] if received is None else [received]
    return pl.pallas_call(
        body,
        grid_spec=pltpu.PrefetchScalarGridSpec(
            num_scalar_prefetch=1,
            grid=(parts * tiles,),
            in_specs=[
                pl.BlockSpec((tokens, count), lambda j, half_ref: (0, half_ref[0])),
                pl.BlockSpec((1, tokens, tile), lambda j, half_ref: (j // tiles, 0, j % tiles)),
            ]
            + [block] * len(more),
            out_specs=block,
            scratch_shapes=[pltpu.VMEM((count, tokens), jnp.bfloat16)],
        ),
        out_shape=shape,
        cost_estimate=cost_of(2 * tokens * count * parts * columns, stack, shape, *more),
    )(half[None], left, stack, *more)


def feed_forward(hidden, gate_up_all):
    rows, depth = hidden.shape
    wide = gate_up_all.shape[1] // 2
    tile = tile_of(wide)

    def body(hidden_ref, gate_ref, up_ref, gate_out, up_out, active_out):
        def step(at):
            gate_part = plain_dot(hidden_ref[at, :], gate_ref[...])
            upward = plain_dot(hidden_ref[at, :], up_ref[...])
            gate_out[at, :] = gate_part
            up_out[at, :] = upward
            active_out[at, :] = (gate_part * jax.nn.sigmoid(gate_part) * upward).astype(jnp.bfloat16)

        by_rows(rows, step)

    block = pl.BlockSpec((rows, tile), lambda j: (0, j))
    kinds = (jnp.float32, jnp.float32, jnp.bfloat16)
    shapes = [jax.ShapeDtypeStruct((rows, wide), kind) for kind in kinds]
    return pl.pallas_call(
        body,
        grid=(wide // tile,),
        in_specs=[
            pl.BlockSpec((rows, depth), lambda j: (0, 0)),
            pl.BlockSpec((depth, tile), lambda j: (0, j)),
            pl.BlockSpec((depth, tile), lambda j: (0, j + wide // tile)),
        ],
        out_specs=[block] * 3,
        out_shape=shapes,
        cost_estimate=cost_of(4 * rows * depth * wide, gate_up_all, *shapes),
    )(hidden, gate_up_all, gate_up_all)


def feed_forward_back(cot, down_all, gate_part, upward):
    rows, depth = cot.shape
    wide = down_all.shape[1]
    tile = tile_of(wide, wide // 2)

    def body(cot_ref, down_ref, gate_ref, up_ref, out_ref):
        def step(at):
            grad_act = plain_dot(cot_ref[at, :], down_ref[...])
            gate = gate_ref[at, :]
            sigmoid_gate = jax.nn.sigmoid(gate)
            slope = sigmoid_gate * (1.0 + gate * (1.0 - sigmoid_gate))
            out_ref[0, at, :] = (grad_act * up_ref[at, :] * slope).astype(jnp.bfloat16)
            out_ref[1, at, :] = (grad_act * (gate * sigmoid_gate)).astype(jnp.bfloat16)

        by_rows(rows, step)

    block = pl.BlockSpec((rows, tile), lambda j: (0, j))
    shape = jax.ShapeDtypeStruct((2, rows, wide), jnp.bfloat16)
    return pl.pallas_call(
        body,
        grid=(wide // tile,),
        in_specs=[
            pl.BlockSpec((rows, depth), lambda j: (0, 0)),
            pl.BlockSpec((depth, tile), lambda j: (0, j)),
            block,
            block,
        ],
        out_specs=pl.BlockSpec((2, rows, tile), lambda j: (0, 0, j)),
        out_shape=shape,
        cost_estimate=cost_of(2 * rows * depth * wide, down_all, gate_part, upward, shape),
    )(cot, down_all, gate_part, upward)


def adam_step(parameter, gradient, first_moment, second_moment):
    new_first = beta_one * first_moment + (1.0 - beta_one) * gradient
    new_second = beta_two * second_moment + (1.0 - beta_two) * gradient * gradient
    corrected_first = new_first / (1.0 - beta_one**step_count)
    corrected_second = new_second / (1.0 - beta_two**step_count)
    new_parameter = parameter - lr_rate * (
        corrected_first / (jnp.sqrt(corrected_second) + adam_eps) + decay_rate * parameter
    )
    return (new_parameter, new_first, new_second)


def adam_update(gradient, parameters, firsts, seconds):
    rows = gradient.shape[0]
    chunk = min(rows, 16)
    count = len(parameters)

    def body(gradient_ref, *refs):
        old, new = refs[: 3 * count], refs[3 * count :]
        begin = 0
        for at in range(count):
            shape = old[3 * at].shape
            middle = range(shape[1]) if len(shape) == 3 else (None,)
            for part in middle:
                wide = shape[-1]
                where = (slice(None), slice(None)) if part is None else (slice(None), part, slice(None))
                grads = gradient_ref[:, begin : begin + wide].astype(jnp.float32)
                begin += wide
                results = adam_step(
                    old[3 * at][where], grads, old[3 * at + 1][where], old[3 * at + 2][where]
                )
                new[4 * at][where] = grads
                for index, result in enumerate(results):
                    new[4 * at + 1 + index][where] = result

    def spec(array):
        return pl.BlockSpec(
            (chunk,) + array.shape[1:], lambda i, zeros=(0,) * (array.ndim - 1): (i,) + zeros
        )

    inputs = [array for group in zip(parameters, firsts, seconds) for array in group]
    outputs = [array for array in parameters for _ in range(4)]
    results = pl.pallas_call(
        body,
        grid=(rows // chunk,),
        in_specs=[spec(gradient)] + [spec(array) for array in inputs],
        out_specs=[spec(array) for array in outputs],
        out_shape=[jax.ShapeDtypeStruct(array.shape, jnp.float32) for array in outputs],
        cost_estimate=cost_of(20 * gradient.size, *inputs, *outputs),
    )(gradient, *inputs)
    return [results[4 * at : 4 * at + 4] for at in range(count)]


def make_shards(dp_size):
    order = ring_order(dp_size)
    inverse_order = [order.index(i) for i in range(dp_size)]
    chips = dp_size // 2
    rings = [order[:chips], order[chips:]]

    def gather(values):
        return lax.all_gather(values, "dp", axis=0, tiled=True, axis_index_groups=[order])

    def scatter(values):
        return lax.psum_scatter(
            values, "dp", scatter_dimension=0, tiled=True, axis_index_groups=rings
        )

    def swap_core(values):
        return lax.ppermute(values, "dp", [(i, i ^ 1) for i in range(dp_size)])

    def pair_grad(left, right):
        core = lax.axis_index("dp") % 2
        other = turned_times(left, 1 - core, right)
        received = swap_core(other)
        return turned_times(left, core, right, received)

    def swap(values):
        return lax.ppermute(values, "tensor", [(0, 1), (1, 0)])

    def gather_small(values):
        at = lax.axis_index("dp")
        place = jnp.asarray(inverse_order, jnp.int32)[at]
        slots = lax.broadcasted_iota(jnp.int32, (1, dp_size, 1), 1) == place
        total = jnp.where(slots, values[:, None, :], jnp.zeros((), values.dtype))
        step = 1
        while step < dp_size:
            total = total + lax.ppermute(total, "dp", [(i, i ^ step) for i in range(dp_size)])
            step *= 2
        return total.reshape(values.shape[0], -1)

    def shards(
        block_input,
        segment_ids,
        cotangent,
        attn_gain,
        query_weight,
        key_value_weight,
        out_weight,
        feed_gain,
        gate_up_weight,
        down_weight,
        *moments,
    ):
        bf16, f32 = jnp.bfloat16, jnp.float32
        rows = attn_gain.shape[0]
        own = block_input.shape[0]
        heads_wide = query_weight.shape[1]
        keys_wide = key_value_weight.shape[2]
        tensor_at = lax.axis_index("tensor")

        qkv_wide = heads_wide + 2 * keys_wide
        gains = gather_small(jnp.stack([attn_gain, feed_gain]).astype(bf16)).astype(f32)
        attn_all = gather(
            jnp.concatenate(
                [query_weight.astype(bf16), key_value_weight.astype(bf16).reshape(rows, -1), out_weight.astype(bf16)],
                axis=1,
            )
        )
        gate_up_all = gather(gate_up_weight.astype(bf16).reshape(rows, -1))
        down_all = gather(down_weight.astype(bf16))
        gain_one, gain_two = gains[0:1], gains[1:2]

        block_rows = permute_blocks(block_input, order)
        cot_own = permute_blocks(cotangent, order)
        segments = segment_ids[0]
        cosine_table, sine_table = rotary_tables(segments, HEAD_DIM, tensor_at * own)

        def both(values):
            return jnp.concatenate([values, swap(values)], axis=0)

        def summed(left, right, first):
            partial = times_turned(left, 1, right, first, bf16)
            theirs = swap(partial)
            mine = times_turned(left, 0, right, first, f32)
            return mine + theirs.astype(f32)

        normed_one, inverse_one = norm_parts(block_rows)
        hidden_one = both((normed_one * gain_one).astype(bf16))
        cot_rows = both(cot_own.astype(bf16))

        qkv = times(hidden_one, attn_all, 0, qkv_wide, f32)
        attn_cat, *saved = attend(
            tensor_at, qkv, cosine_table, sine_table, segments, heads_wide
        )

        residual = block_rows + summed(attn_cat, attn_all, qkv_wide)
        normed_two, inverse_two = norm_parts(residual)
        hidden_two = both((normed_two * gain_two).astype(bf16))
        gate_part, upward, activated = feed_forward(hidden_two, gate_up_all)
        down_grad = pair_grad(cot_rows, activated)
        down_grad, down_all = lax.optimization_barrier((down_grad, down_all))
        down_sum = scatter(down_grad)
        grad_gate_up = feed_forward_back(cot_rows, down_all, gate_part, upward)
        grad_hidden_two = summed(grad_gate_up, gate_up_all, 0)
        gate_up_grad = pair_grad(hidden_two, grad_gate_up)
        gate_up_sum = scatter(gate_up_grad)
        feed_sum = summed(activated, down_all, 0)
        block_output = lax.optimization_barrier(residual) + feed_sum
        grad_residual = cot_own + norm_back(grad_hidden_two, gain_two, normed_two, inverse_two)
        feed_gain_part = jnp.sum(grad_hidden_two * normed_two, axis=0)
        grad_rows = both(grad_residual.astype(bf16))
        out_grad = pair_grad(grad_rows, attn_cat)
        grad_cat = times(grad_rows, attn_all, qkv_wide, heads_wide, bf16)
        grad_qkv = attend_back(
            tensor_at, grad_cat, saved, cosine_table, sine_table, segments
        )
        grad_hidden_one = summed(grad_qkv, attn_all, 0)
        qkv_grad = pair_grad(hidden_one, grad_qkv)
        input_grad = grad_residual + norm_back(grad_hidden_one, gain_one, normed_one, inverse_one)
        attn_gain_part = jnp.sum(grad_hidden_one * normed_one, axis=0)

        parts = [rows_major(qkv_grad), rows_major(out_grad)]
        attn_sum = rows_major(scatter(jnp.concatenate(parts, axis=1)))
        gain_parts = jnp.stack([attn_gain_part, feed_gain_part])
        gain_parts = gain_parts + swap(gain_parts)
        step = 1
        while step < dp_size:
            pairs = [(i, i ^ step) for i in range(dp_size)]
            gain_parts = gain_parts + lax.ppermute(gain_parts, "dp", pairs)
            step *= 2
        place = jnp.asarray(inverse_order, jnp.int32)[lax.axis_index("dp")]
        gain_sums = lax.dynamic_slice(gain_parts, (0, place * rows), (2, rows))
        attn_gain_sum, feed_gain_sum = gain_sums[0], gain_sums[1]

        count = len(moments) // 2
        firsts, seconds = moments[:count], moments[count:]

        def update(gradient, parameters, places):
            results = adam_update(gradient, parameters, [firsts[at] for at in places], [seconds[at] for at in places])
            return dict(zip(places, results))

        attn_parameters = (query_weight, key_value_weight, out_weight)
        results = update(down_sum, (down_weight,), (6,))
        results |= update(gate_up_sum, (gate_up_weight,), (5,))
        results |= update(attn_sum, attn_parameters, (1, 2, 3))
        for at, parameter, gradient in (
            (0, attn_gain, attn_gain_sum),
            (4, feed_gain, feed_gain_sum),
        ):
            results[at] = (gradient, *adam_step(parameter, gradient, firsts[at], seconds[at]))
        return (
            permute_blocks(block_output, inverse_order),
            permute_blocks(input_grad, inverse_order),
        ) + tuple(results[at][kind] for kind in range(4) for at in range(count))

    return shards


def solution(mesh):
    tokens = P(("dp", "tensor"), None)
    gain = P("dp")
    flat = P("dp", "tensor")
    paired = P("dp", None, "tensor")
    weights = (gain, flat, paired, flat, gain, paired, flat)
    shards = make_shards(mesh.shape["dp"])

    return jax.shard_map(
        shards,
        mesh=mesh,
        in_specs=(tokens, P("dp", None), tokens) + weights * 3,
        out_specs=(tokens, tokens) + weights * 4,
        check_vma=False,
    )
```

profile of v0, /device:TPU:0, one launch (start us, length us, event | category | flops | bytes accessed | tf_op | source)
XLA Modules:
  0.0 602.5 jit_solution(10722593226029216633)
XLA Ops:
  43.6 16.5 %collective-permute-done.4 = bf16[256,2048]{1,0:T(8,128)(2,1)} collective-permute-done((bf16[256,2048]{1,0:T(8,128)(2,1)S(1)}, bf16[256,2048]{1,0:T(8,128)(2,1)}, u32[]{:S(2)}, u32[]{:S(2)}) %collective-permute-start.4) | collective-permute-done | bytes 1048608 | tf_op jit(solution)/shard_map/ppermute | solution.py:614
  77.2 16.8 %shard_map.483 = (bf16[512,1024]{1,0:T(8,128)(2,1)}, bf16[512,1024]{1,0:T(8,128)(2,1)}, bf16[2,2,512,128]{3,2,1,0:T(8,128)(2,1)}, bf16[512,128]{1,0:T(8,128)(2,1...) custom-call(s32[1]{0:T(128)} %bitcast.at_ref, f32[512,1280]{1,0:T(8,128)} %shard_map.482.qkv_ref, ...), custom_call_target="tpu_custom_call" | custom-call | flops 1073741824 | bytes 5242880 | tf_op jit(solution)/shard_map/pallas_call | solution.py:303
  114.4 12.1 %collective-permute-done.5 = bf16[256,2048]{1,0:T(8,128)(2,1)} collective-permute-done((bf16[256,2048]{1,0:T(8,128)(2,1)}, bf16[256,2048]{1,0:T(8,128)(2,1)}, u32[]{:S(2)}, u32[]{:S(2)}) %collective-permute-start.5) | collective-permute-done | bytes 1048608 | tf_op jit(solution)/shard_map/ppermute | solution.py:614
  133.3 15.7 %collective-permute-done.7 = bf16[256,2048]{1,0:T(8,128)(2,1)} collective-permute-done((bf16[256,2048]{1,0:T(8,128)(2,1)S(1)}, bf16[256,2048]{1,0:T(8,128)(2,1)}, u32[]{:S(2)}, u32[]{:S(2)}) %collective-permute-start.7) | collective-permute-done | bytes 1048608 | tf_op jit(solution)/shard_map/ppermute | solution.py:614
  151.7 19.2 %collective-permute-done.6 = bf16[256,2048]{1,0:T(8,128)(2,1)} collective-permute-done((bf16[256,2048]{1,0:T(8,128)(2,1)}, bf16[256,2048]{1,0:T(8,128)(2,1)}, u32[]{:S(2)}, u32[]{:S(2)}) %collective-permute-start.6) | collective-permute-done | bytes 1048608 | tf_op jit(solution)/shard_map/ppermute | solution.py:614
  174.0 15.7 %all-gather.6.cloned.1.call-done.gate_ref.up_ref.right_ref = bf16[2048,5632]{1,0:T(8,128)(2,1)} async-done(((bf16[128,5632]{1,0:T(8,128)(2,1)}), bf16[2048,5632]{1,0:T(8,128)(2,1)}) %all-gather.6.cloned.1.call-update) | async-done | bytes 23068688 | tf_op jit(solution)/shard_map/all_gather | solution.py:597
  189.8 22.7 %shard_map.486 = (f32[512,2816]{1,0:T(8,128)}, f32[512,2816]{1,0:T(8,128)}, bf16[512,2816]{1,0:T(8,128)(2,1)}) custom-call(bf16[512,2048]{1,0:T(8,128)(2,1)} %pad_maximum_fusion.2.hidden_ref.left_ref, bf16[2048,5632]{1,0:T(8,128)(2,1)} %all-gather.6.cloned.1.call-done.gate_ref.up_ref.right_ref, ...), custom_call_target="tpu_custom_call" | custom-call | flops 11811160064 | bytes 37486592 | tf_op jit(solution)/shard_map/pallas_call | solution.py:491
  212.4 8.9 %shard_map.488 = bf16[1024,2816]{1,0:T(8,128)(2,1)} custom-call(s32[1]{0:T(128)} %bitcast.11.half_ref, bf16[512,2048]{1,0:T(8,128)(2,1)} %pad_maximum_fusion.3.left_ref.cot_ref, bf16[1,512,2816]{2,1,0:T(8,128)(2,1)} %bitcast.36), custom_call_target="tpu_custom_call" | custom-call | flops 2952790016 | bytes 8650752 | tf_op jit(solution)/shard_map/pallas_call | solution.py:455
  221.5 10.9 %collective-permute-done.8.rest_0_ = bf16[1024,2816]{1,0:T(8,128)(2,1)} collective-permute-done((bf16[1024,2816]{1,0:T(8,128)(2,1)}, bf16[1024,2816]{1,0:T(8,128)(2,1)}, u32[]{:S(2)}, u32[]{:S(2)}) %collective-permute-start.8) | collective-permute-done | bytes 5767200 | tf_op jit(solution)/shard_map/ppermute | solution.py:605
  232.4 9.8 %shard_map.489 = bf16[1024,2816]{1,0:T(8,128)(2,1)} custom-call(s32[1]{0:T(128)} %bitcast.10.half_ref, bf16[512,2048]{1,0:T(8,128)(2,1)} %pad_maximum_fusion.3.left_ref.cot_ref, bf16[1,512,2816]{2,1,0:T(8,128)(2,1)} %bitcast.37, bf16[1024,2816]{1,0:T(8,128)(2,1)} %collective-permute-done.8.rest_0_), custom_call_target="tpu_custom_call" | custom-call | flops 2952790016 | bytes 14417920 | tf_op jit(solution)/shard_map/pallas_call | solution.py:455
  242.2 13.6 %all-gather.8.cloned.1.call-done.right_ref.down_ref = bf16[2048,2816]{1,0:T(8,128)(2,1)} async-done(((bf16[128,2816]{1,0:T(8,128)(2,1)}), bf16[2048,2816]{1,0:T(8,128)(2,1)}) %all-gather.8.cloned.1.call-update) | async-done | bytes 11534352 | tf_op jit(solution)/shard_map/all_gather | solution.py:597
  256.0 15.1 %shard_map.493.left_ref.right_ref = bf16[2,512,2816]{2,1,0:T(8,128)(2,1)} custom-call(bf16[512,2048]{1,0:T(8,128)(2,1)} %pad_maximum_fusion.3.left_ref.cot_ref, bf16[2048,2816]{1,0:T(8,128)(2,1)} %all-gather.8.cloned.1.call-done.right_ref.down_ref, f32[512,2816]{1,0:T(8,128)} %get-tuple-element.64.gate_ref, f32[512,2816]{1,0:T(8,128)} %get-tuple-element.65.up_ref), custom_call_target="tpu_custom_call" | custom-call | flops 5905580032 | bytes 28835840 | tf_op jit(solution)/shard_map/pallas_call | solution.py:523
  271.1 12.5 %shard_map.495 = bf16[256,2048]{1,0:T(8,128)(2,1)} custom-call(bf16[2,512,2816]{2,1,0:T(8,128)(2,1)} %shard_map.493.left_ref.right_ref, bf16[2048,5632]{1,0:T(8,128)(2,1)} %all-gather.6.cloned.1.call-done.gate_ref.up_ref.right_ref), custom_call_target="tpu_custom_call" | custom-call | flops 5905580032 | bytes 24117248 | tf_op jit(solution)/shard_map/pallas_call | solution.py:412
  285.1 12.8 %shard_map.494 = f32[256,2048]{1,0:T(8,128)} custom-call(bf16[2,512,2816]{2,1,0:T(8,128)(2,1)} %shard_map.493.left_ref.right_ref, bf16[2048,5632]{1,0:T(8,128)(2,1)} %all-gather.6.cloned.1.call-done.gate_ref.up_ref.right_ref), custom_call_target="tpu_custom_call" | custom-call | flops 5905580032 | bytes 25165824 | tf_op jit(solution)/shard_map/pallas_call | solution.py:412
  297.9 11.3 %collective-permute-done.10 = bf16[256,2048]{1,0:T(8,128)(2,1)S(1)} collective-permute-done((bf16[256,2048]{1,0:T(8,128)(2,1)}, bf16[256,2048]{1,0:T(8,128)(2,1)S(1)}, u32[]{:S(2)}, u32[]{:S(2)}) %collective-permute-start.10) | collective-permute-done | bytes 1048608 | tf_op jit(solution)/shard_map/ppermute | solution.py:614
  318.1 22.4 %collective-permute-done.11 = bf16[256,2048]{1,0:T(8,128)(2,1)S(1)} collective-permute-done((bf16[256,2048]{1,0:T(8,128)(2,1)S(1)}, bf16[256,2048]{1,0:T(8,128)(2,1)S(1)}, u32[]{:S(2)}, u32[]{:S(2)}) %collective-permute-start.11) | collective-permute-done | bytes 1048608 | tf_op jit(solution)/shard_map/ppermute | solution.py:614
  348.8 16.9 %shard_map.497 = bf16[512,1280]{1,0:T(8,128)(2,1)} custom-call(s32[1]{0:T(128)} %bitcast.at_ref, bf16[512,1024]{1,0:T(8,128)(2,1)} %shard_map.496.grad_ref, bf16[512,1024]{1,0:T(8,128)(2,1)} %get-tuple-element.66.query_ref, bf16[2,2,512,128]{3,2,1,0:T(8,128)(2,1)} %get-tuple-element.67.side_ref, bf16[512,128]{1,0:T(8,128)(2,1)} %get-tuple-element.68.key_ref, ...), custom_call_target="tpu_custom_call" | custom-call | flops 2684354560 | bytes 4194304 | tf_op jit(solution)/shard_map/pallas_call | solution.py:320
  378.3 13.6 %shard_map.506 = bf16[1024,5632]{1,0:T(8,128)(2,1)} custom-call(s32[1]{0:T(128)} %bitcast.11.half_ref, bf16[512,2048]{1,0:T(8,128)(2,1)} %pad_maximum_fusion.2.hidden_ref.left_ref, bf16[2,512,2816]{2,1,0:T(8,128)(2,1)} %shard_map.493.left_ref.right_ref), custom_call_target="tpu_custom_call" | custom-call | flops 5905580032 | bytes 17301504 | tf_op jit(solution)/shard_map/pallas_call | solution.py:455
  410.0 15.6 %shard_map.507 = bf16[1024,5632]{1,0:T(8,128)(2,1)} custom-call(s32[1]{0:T(128)} %bitcast.10.half_ref, bf16[512,2048]{1,0:T(8,128)(2,1)} %pad_maximum_fusion.2.hidden_ref.left_ref, bf16[2,512,2816]{2,1,0:T(8,128)(2,1)} %shard_map.493.left_ref.right_ref, bf16[1024,5632]{1,0:T(8,128)(2,1)} %collective-permute-done.20.rest_0_), custom_call_target="tpu_custom_call" | custom-call | flops 5905580032 | bytes 28835840 | tf_op jit(solution)/shard_map/pallas_call | solution.py:455
  440.8 17.0 %collective-permute-done.12 = bf16[256,2048]{1,0:T(8,128)(2,1)S(1)} collective-permute-done((bf16[256,2048]{1,0:T(8,128)(2,1)}, bf16[256,2048]{1,0:T(8,128)(2,1)S(1)}, u32[]{:S(2)}, u32[]{:S(2)}) %collective-permute-start.12) | collective-permute-done | bytes 1048608 | tf_op jit(solution)/shard_map/ppermute | solution.py:614
  470.3 9.2 %shard_map.490 = f32[256,2048]{1,0:T(8,128)} custom-call(bf16[1,512,2816]{2,1,0:T(8,128)(2,1)} %bitcast.39, bf16[2048,2816]{1,0:T(8,128)(2,1)} %all-gather.8.cloned.1.call-done.right_ref.down_ref), custom_call_target="tpu_custom_call" | custom-call | flops 2952790016 | bytes 13631488 | tf_op jit(solution)/shard_map/pallas_call | solution.py:412
  480.6 13.9 %collective-permute-done.9 = bf16[256,2048]{1,0:T(8,128)(2,1)} collective-permute-done((bf16[256,2048]{1,0:T(8,128)(2,1)}, bf16[256,2048]{1,0:T(8,128)(2,1)}, u32[]{:S(2)}, u32[]{:S(2)}) %collective-permute-start.9) | collective-permute-done | bytes 1048608 | tf_op jit(solution)/shard_map/ppermute | solution.py:614
  533.5 50.4 %reduce-scatter.6.cloned.1.call-done.gradient_ref = bf16[128,5632]{1,0:T(8,128)(2,1)} async-done(((bf16[1024,5632]{1,0:T(8,128)(2,1)}), bf16[128,5632]{1,0:T(8,128)(2,1)}) %reduce-scatter.6.cloned.1.call-update) | async-done | bytes 1441808 | tf_op jit(solution)/shard_map/reduce_scatter | solution.py:600
  583.9 11.7 %shard_map.508 = (f32[128,2,2816]{2,1,0:T(2,128)}, f32[128,2,2816]{2,1,0:T(2,128)}, f32[128,2,2816]{2,1,0:T(2,128)}, f32[128,2,2816]{2,1,0:T(2,128)}) custom-call(bf16[128,5632]{1,0:T(8,128)(2,1)} %reduce-scatter.6.cloned.1.call-done.gradient_ref, f32[128,2,2816]{2,1,0:T(2,128)} %refs_0_.4, f32[128,2,2816]{2,1,0:T(2,128)} %refs_1_.4, f32[128,2,2816]{2,1,0:T(2,128)} %refs_2_.4), custom_call_target="tpu_custom_call" | custom-call | flops 14417920 | bytes 20185088 | tf_op jit(solution)/shard_map/pallas_call | solution.py:579
  (148 shorter events, 203.3 us)
Async XLA Ops:
  7.2 61.7 %all-gather.4.cloned.1.call-start = ((), (), s32[]{:S(2)}) async-start(), calls=%async_computation.3 | async-start | bytes 10027008 | tf_op jit(solution)/shard_map/all_gather | solution.py:597
  11.3 178.5 %all-gather.6.cloned.1.call-start = ((), (), s32[]{:S(2)}) async-start(), calls=%async_computation.4 | async-start | bytes 24510464 | tf_op jit(solution)/shard_map/all_gather | solution.py:597
  15.4 240.3 %all-gather.8.cloned.1.call-start = ((), (), s32[]{:S(2)}) async-start(), calls=%async_computation.5 | async-start | bytes 12255232 | tf_op jit(solution)/shard_map/all_gather | solution.py:597
  17.0 501.3 %reduce-scatter.8.cloned.1.call-start = ((), (), s32[]{:S(2)}) async-start(), calls=%async_computation.8 | async-start | bytes 6488064 | tf_op jit(solution)/shard_map/reduce_scatter | solution.py:600
  22.8 4.5 collective-permute-start.1
  31.3 4.9 collective-permute-start.3
  36.4 23.7 %collective-permute-start.4 = (bf16[256,2048]{1,0:T(8,128)(2,1)S(1)}, bf16[256,2048]{1,0:T(8,128)(2,1)}, u32[]{:S(2)}, u32[]{:S(2)}) collective-permute-start(bf16[256,2048]{1,0:T(8,128)(2,1)S(1)} %multiply_convert_fusion.1), channel_id=1, source_target_pairs={{0,1},{1,0},{2,3},{3,2},{4,5},{5,4},{6,7},{7,6},{8,9},{9,8},{10,11... | collective-permute-start | bytes 3145736 | tf_op jit(solution)/shard_map/ppermute | solution.py:614
  100.1 26.3 %collective-permute-start.5 = (bf16[256,2048]{1,0:T(8,128)(2,1)}, bf16[256,2048]{1,0:T(8,128)(2,1)}, u32[]{:S(2)}, u32[]{:S(2)}) collective-permute-start(bf16[256,2048]{1,0:T(8,128)(2,1)} %shard_map.485), channel_id=1, source_target_pairs={{0,1},{1,0},{2,3},{3,2},{4,5},{5,4},{6,7},{7,6},{8,9},{9,8},{10,11... | collective-permute-start | bytes 3145736 | tf_op jit(solution)/shard_map/ppermute | solution.py:614
  107.5 41.4 %collective-permute-start.7 = (bf16[256,2048]{1,0:T(8,128)(2,1)S(1)}, bf16[256,2048]{1,0:T(8,128)(2,1)}, u32[]{:S(2)}, u32[]{:S(2)}) collective-permute-start(bf16[256,2048]{1,0:T(8,128)(2,1)S(1)} %convert_element_type.68), channel_id=1, source_target_pairs={{0,1},{1,0},{2,3},{3,2},{4,5},{5,4},{6,7},{7,6},{8,9},{9,8},{10,11... | collective-permute-start | bytes 3145736 | tf_op jit(solution)/shard_map/ppermute | solution.py:614
  131.5 39.4 %collective-permute-start.6 = (bf16[256,2048]{1,0:T(8,128)(2,1)}, bf16[256,2048]{1,0:T(8,128)(2,1)}, u32[]{:S(2)}, u32[]{:S(2)}) collective-permute-start(bf16[256,2048]{1,0:T(8,128)(2,1)} %multiply_convert_fusion), channel_id=1, source_target_pairs={{0,1},{1,0},{2,3},{3,2},{4,5},{5,4},{6,7},{7,6},{8,9},{9,8},{10,11... | collective-permute-start | bytes 3145736 | tf_op jit(solution)/shard_map/ppermute | solution.py:614
  221.3 11.0 %collective-permute-start.8 = (bf16[1024,2816]{1,0:T(8,128)(2,1)}, bf16[1024,2816]{1,0:T(8,128)(2,1)}, u32[]{:S(2)}, u32[]{:S(2)}) collective-permute-start(bf16[1024,2816]{1,0:T(8,128)(2,1)} %shard_map.488), channel_id=1, source_target_pairs={{0,2},{2,0},{4,6},{6,4},{8,10},{10,8},{12,14},{14,12},{16,18},{18,... | collective-permute-start | bytes 17301512 | tf_op jit(solution)/shard_map/ppermute | solution.py:605
  255.8 270.5 %reduce-scatter.4.cloned.1.call-start = ((), (), s32[]{:S(2)}) async-start(), calls=%async_computation.6 | async-start | bytes 5308416 | tf_op jit(solution)/shard_map/reduce_scatter | solution.py:600
  283.6 25.5 %collective-permute-start.10 = (bf16[256,2048]{1,0:T(8,128)(2,1)}, bf16[256,2048]{1,0:T(8,128)(2,1)S(1)}, u32[]{:S(2)}, u32[]{:S(2)}) collective-permute-start(bf16[256,2048]{1,0:T(8,128)(2,1)} %shard_map.495), channel_id=1, source_target_pairs={{0,1},{1,0},{2,3},{3,2},{4,5},{5,4},{6,7},{7,6},{8,9},{9,8},{10,11... | collective-permute-start | bytes 3145736 | tf_op jit(solution)/shard_map/ppermute | solution.py:614
  315.9 24.6 %collective-permute-start.11 = (bf16[256,2048]{1,0:T(8,128)(2,1)S(1)}, bf16[256,2048]{1,0:T(8,128)(2,1)S(1)}, u32[]{:S(2)}, u32[]{:S(2)}) collective-permute-start(bf16[256,2048]{1,0:T(8,128)(2,1)S(1)} %get-tuple-element.104), channel_id=1, source_target_pairs={{0,1},{1,0},{2,3},{3,2},{4,5},{5,4},{6,7},{7,6},{8,9},{9,8},{10,11... | collective-permute-start | bytes 3145736 | tf_op jit(solution)/shard_map/ppermute | solution.py:614
  372.0 26.0 %collective-permute-start.18 = (bf16[1024,1280]{1,0:T(8,128)(2,1)}, bf16[1024,1280]{1,0:T(8,128)(2,1)}, u32[]{:S(2)}, u32[]{:S(2)}) collective-permute-start(bf16[1024,1280]{1,0:T(8,128)(2,1)} %shard_map.501), channel_id=1, source_target_pairs={{0,2},{2,0},{4,6},{6,4},{8,10},{10,8},{12,14},{14,12},{16,18},{18,... | collective-permute-start | bytes 7864328 | tf_op jit(solution)/shard_map/ppermute | solution.py:605
  377.8 14.1 %collective-permute-start.19 = (bf16[1024,1024]{1,0:T(8,128)(2,1)}, bf16[1024,1024]{1,0:T(8,128)(2,1)}, u32[]{:S(2)}, u32[]{:S(2)}) collective-permute-start(bf16[1024,1024]{1,0:T(8,128)(2,1)} %shard_map.503), channel_id=1, source_target_pairs={{0,2},{2,0},{4,6},{6,4},{8,10},{10,8},{12,14},{14,12},{16,18},{18,... | collective-permute-start | bytes 6291464 | tf_op jit(solution)/shard_map/ppermute | solution.py:605
  391.9 18.1 %collective-permute-start.20 = (bf16[1024,5632]{1,0:T(8,128)(2,1)}, bf16[1024,5632]{1,0:T(8,128)(2,1)}, u32[]{:S(2)}, u32[]{:S(2)}) collective-permute-start(bf16[1024,5632]{1,0:T(8,128)(2,1)} %shard_map.506), channel_id=1, source_target_pairs={{0,2},{2,0},{4,6},{6,4},{8,10},{10,8},{12,14},{14,12},{16,18},{18,... | collective-permute-start | bytes 34603016 | tf_op jit(solution)/shard_map/ppermute | solution.py:605
  409.7 174.3 %reduce-scatter.6.cloned.1.call-start = ((), (), s32[]{:S(2)}) async-start(), calls=%async_computation.7 | async-start | bytes 12976128 | tf_op jit(solution)/shard_map/reduce_scatter | solution.py:600
  432.0 25.8 %collective-permute-start.12 = (bf16[256,2048]{1,0:T(8,128)(2,1)}, bf16[256,2048]{1,0:T(8,128)(2,1)S(1)}, u32[]{:S(2)}, u32[]{:S(2)}) collective-permute-start(bf16[256,2048]{1,0:T(8,128)(2,1)} %shard_map.499), channel_id=1, source_target_pairs={{0,1},{1,0},{2,3},{3,2},{4,5},{5,4},{6,7},{7,6},{8,9},{9,8},{10,11... | collective-permute-start | bytes 3145736 | tf_op jit(solution)/shard_map/ppermute | solution.py:614
  460.1 10.1 %collective-permute-start.13 = (f32[2,2048]{1,0:T(2,128)S(1)}, f32[2,2048]{1,0:T(2,128)S(1)}, u32[]{:S(2)}, u32[]{:S(2)}) collective-permute-start(f32[2,2048]{1,0:T(2,128)S(1)} %pad_maximum_fusion.7), channel_id=1, source_target_pairs={{0,1},{1,0},{2,3},{3,2},{4,5},{5,4},{6,7},{7,6},{8,9},{9,8},{10,11... | collective-permute-start | bytes 49160 | tf_op jit(solution)/shard_map/ppermute | solution.py:614
  469.7 24.8 %collective-permute-start.9 = (bf16[256,2048]{1,0:T(8,128)(2,1)}, bf16[256,2048]{1,0:T(8,128)(2,1)}, u32[]{:S(2)}, u32[]{:S(2)}) collective-permute-start(bf16[256,2048]{1,0:T(8,128)(2,1)} %shard_map.491), channel_id=1, source_target_pairs={{0,1},{1,0},{2,3},{3,2},{4,5},{5,4},{6,7},{7,6},{8,9},{9,8},{10,11... | collective-permute-start | bytes 3145736 | tf_op jit(solution)/shard_map/ppermute | solution.py:614
  470.2 9.3 %collective-permute-start.14 = (f32[2,2048]{1,0:T(2,128)S(1)}, f32[2,2048]{1,0:T(2,128)S(1)}, u32[]{:S(2)}, u32[]{:S(2)}) collective-permute-start(f32[2,2048]{1,0:T(2,128)S(1)} %fusion.6), channel_id=1, source_target_pairs={{0,2},{2,0},{4,6},{6,4},{8,10},{10,8},{12,14},{14,12},{16,18},{18,... | collective-permute-start | bytes 49160 | tf_op jit(solution)/shard_map/ppermute | solution.py:715
  479.5 23.4 %collective-permute-start.15 = (f32[2,2048]{1,0:T(2,128)S(1)}, f32[2,2048]{1,0:T(2,128)S(1)}, u32[]{:S(2)}, u32[]{:S(2)}) collective-permute-start(f32[2,2048]{1,0:T(2,128)S(1)} %fusion.11), channel_id=1, source_target_pairs={{0,4},{2,6},{4,0},{6,2},{8,12},{10,14},{12,8},{14,10},{16,20},{18,... | collective-permute-start | bytes 49160 | tf_op jit(solution)/shard_map/ppermute | solution.py:715
  507.2 10.5 %collective-permute-start.17 = (f32[2,2048]{1,0:T(2,128)S(1)}, f32[2,2048]{1,0:T(2,128)S(1)}, u32[]{:S(2)}, u32[]{:S(2)}) collective-permute-start(f32[2,2048]{1,0:T(2,128)S(1)} %add.130), channel_id=1, source_target_pairs={{0,16},{2,18},{4,20},{6,22},{8,24},{10,26},{12,28},{14,30},{16,0},... | collective-permute-start | bytes 49160 | tf_op jit(solution)/shard_map/ppermute | solution.py:715
  (17 other events, 97.4 us)
Sparse Core Ops, SparseCore 0:
  11.4 57.5 all-gather.3
  71.1 118.6 all-gather.5
  191.4 64.3 all-gather.7
  257.9 63.2 reduce-scatter.7
  409.8 53.4 reduce-scatter.3
  465.4 118.4 reduce-scatter.5
where the time goes:
time: 605 us; the launch traced here: 603 us
  Pallas kernels  270 us (45%)
  waiting for transfers between devices  232 us (38%)
  other arithmetic  51.5 us (9%)
  starting transfers between devices  26.7 us (4%)
  between operations  15.1 us (2%)
  local copies, waits for them, and re-layouts  7.96 us (1%)
    ppermute x9, waiting for transfers between devices, swap(): return lax.ppermute(values, 'tensor', [(0, 1), (1, 0)])  128 us
    pallas_call x8, Pallas kernels, turned_times(): pl.pallas_call(body, grid_spec=pltpu.PrefetchScalarGridSpec(num_scalar_pr...  72.9 us
    pallas_call x8, Pallas kernels, times_turned(): pl.pallas_call(body, grid=(count // tile,), in_specs=[pl.BlockSpec((parts...  68.2 us
    reduce_scatter x3, waiting for transfers between devices, scatter(): lax.psum_scatter(values, 'dp', scatter_dimension=0, tiled=True, axis_inde...  50.4 us
    all_gather x3, waiting for transfers between devices, gather(): lax.all_gather(values, 'dp', axis=0, tiled=True, axis_index_groups=[order])  35.3 us
    pallas_call x3, Pallas kernels, adam_update(): pl.pallas_call(body, grid=(rows // chunk,), in_specs=[spec(gradient)] + [...  26.9 us
    pallas_call x1, Pallas kernels, feed_forward(): pl.pallas_call(body, grid=(wide // tile,), in_specs=[pl.BlockSpec((rows,...  22.7 us
    pallas_call x1, Pallas kernels, attend_back(): pl.pallas_call(attend_back_body, in_specs=whole_specs(12), out_specs=pl.B...  16.9 us
  transfers between devices with their start and end apart: 27, of which 17 were waited for; matrix products, arithmetic and copies ran while one was open for 9% of the time, Pallas kernels for 43%

commit v1 on v0

--- a/solution.py
+++ b/solution.py
@@ -546,9 +546,32 @@
     return (new_parameter, new_first, new_second)
 
 
-def adam_update(gradient, parameters, firsts, seconds):
+def pack(*weights):
+    rows = weights[0].shape[0]
+    wide = sum(weight.size // rows for weight in weights)
+
+    def body(*refs):
+        *weight_refs, out_ref = refs
+        begin = 0
+        for ref in weight_refs:
+            for part in range(ref.shape[1]) if len(ref.shape) == 3 else (None,):
+                values = ref[...] if part is None else ref[:, part, :]
+                out_ref[:, begin : begin + ref.shape[-1]] = values.astype(jnp.bfloat16)
+                begin += ref.shape[-1]
+
+    shape = jax.ShapeDtypeStruct((rows, wide), jnp.bfloat16)
+    return pl.pallas_call(
+        body,
+        in_specs=[pl.BlockSpec(memory_space=pltpu.VMEM)] * len(weights),
+        out_specs=pl.BlockSpec(memory_space=pltpu.VMEM),
+        out_shape=shape,
+        cost_estimate=cost_of(shape.size, shape, *weights),
+    )(*weights)
+
+
+def adam_update(gradient, parameters, firsts, seconds, chunk):
     rows = gradient.shape[0]
-    chunk = min(rows, 16)
+    chunk = min(rows, chunk)
     count = len(parameters)
 
     def body(gradient_ref, *refs):
@@ -646,12 +669,7 @@
 
         qkv_wide = heads_wide + 2 * keys_wide
         gains = gather_small(jnp.stack([attn_gain, feed_gain]).astype(bf16)).astype(f32)
-        attn_all = gather(
-            jnp.concatenate(
-                [query_weight.astype(bf16), key_value_weight.astype(bf16).reshape(rows, -1), out_weight.astype(bf16)],
-                axis=1,
-            )
-        )
+        attn_all = gather(pack(query_weight, key_value_weight, out_weight))
         gate_up_all = gather(gate_up_weight.astype(bf16).reshape(rows, -1))
         down_all = gather(down_weight.astype(bf16))
         gain_one, gain_two = gains[0:1], gains[1:2]
@@ -721,14 +739,20 @@
         count = len(moments) // 2
         firsts, seconds = moments[:count], moments[count:]
 
-        def update(gradient, parameters, places):
-            results = adam_update(gradient, parameters, [firsts[at] for at in places], [seconds[at] for at in places])
+        def update(gradient, parameters, places, chunk):
+            results = adam_update(
+                gradient,
+                parameters,
+                [firsts[at] for at in places],
+                [seconds[at] for at in places],
+                chunk,
+            )
             return dict(zip(places, results))
 
         attn_parameters = (query_weight, key_value_weight, out_weight)
-        results = update(down_sum, (down_weight,), (6,))
-        results |= update(gate_up_sum, (gate_up_weight,), (5,))
-        results |= update(attn_sum, attn_parameters, (1, 2, 3))
+        results = update(down_sum, (down_weight,), (6,), 32)
+        results |= update(gate_up_sum, (gate_up_weight,), (5,), 16)
+        results |= update(attn_sum, attn_parameters, (1, 2, 3), 64)
         for at, parameter, gradient in (
             (0, attn_gain, attn_gain_sum),
             (4, feed_gain, feed_gain_sum),

time: 605 us -> 603 us (level)
  transfers between devices with their start and end apart: 27 -> 27, of which waited for: 17 -> 16; matrix products, arithmetic and copies ran while one was open for 9% -> 9% of each run, Pallas kernels for 43% -> 42%
where the time goes in v1:
time: 603 us; the launch traced here: 601 us
  Pallas kernels  267 us (44%)
  waiting for transfers between devices  236 us (39%)
  other arithmetic  47.6 us (8%)
  starting transfers between devices  27 us (4%)
  between operations  15.1 us (3%)
  local copies, waits for them, and re-layouts  7.94 us (1%)
    ppermute x9, waiting for transfers between devices, swap(): return lax.ppermute(values, 'tensor', [(0, 1), (1, 0)])  127 us
    pallas_call x8, Pallas kernels, turned_times(): pl.pallas_call(body, grid_spec=pltpu.PrefetchScalarGridSpec(num_scalar_pr...  72.9 us
    pallas_call x8, Pallas kernels, times_turned(): pl.pallas_call(body, grid=(count // tile,), in_specs=[pl.BlockSpec((parts...  68.2 us
    reduce_scatter x3, waiting for transfers between devices, scatter(): lax.psum_scatter(values, 'dp', scatter_dimension=0, tiled=True, axis_inde...  55 us
    all_gather x3, waiting for transfers between devices, gather(): lax.all_gather(values, 'dp', axis=0, tiled=True, axis_index_groups=[order])  36.1 us
    pallas_call x1, Pallas kernels, feed_forward(): pl.pallas_call(body, grid=(wide // tile,), in_specs=[pl.BlockSpec((rows,...  22.7 us
    pallas_call x3, Pallas kernels, adam_update(): pl.pallas_call(body, grid=(rows // chunk,), in_specs=[spec(gradient)] + [...  22.3 us
    pallas_call x1, Pallas kernels, attend_back(): pl.pallas_call(attend_back_body, in_specs=whole_specs(12), out_specs=pl.B...  16.9 us
  transfers between devices with their start and end apart: 27, of which 16 were waited for; matrix products, arithmetic and copies ran while one was open for 9% of the time, Pallas kernels for 42%

profile of v1, /device:TPU:0, one launch (start us, length us, event | category | flops | bytes accessed | tf_op | source)
XLA Modules:
  0.0 601.3 jit_solution(16152525120341543519)
XLA Ops:
  42.0 16.2 %collective-permute-done.4 = bf16[256,2048]{1,0:T(8,128)(2,1)} collective-permute-done((bf16[256,2048]{1,0:T(8,128)(2,1)S(1)}, bf16[256,2048]{1,0:T(8,128)(2,1)}, u32[]{:S(2)}, u32[]{:S(2)}) %collective-permute-start.4) | collective-permute-done | bytes 1048608 | tf_op jit(solution)/shard_map/ppermute | solution.py:637
  76.0 16.8 %shard_map.484 = (bf16[512,1024]{1,0:T(8,128)(2,1)}, bf16[512,1024]{1,0:T(8,128)(2,1)}, bf16[2,2,512,128]{3,2,1,0:T(8,128)(2,1)}, bf16[512,128]{1,0:T(8,128)(2,1...) custom-call(s32[1]{0:T(128)} %bitcast.at_ref, f32[512,1280]{1,0:T(8,128)} %shard_map.483.qkv_ref, ...), custom_call_target="tpu_custom_call" | custom-call | flops 1073741824 | bytes 5242880 | tf_op jit(solution)/shard_map/pallas_call | solution.py:303
  113.2 12.1 %collective-permute-done.5 = bf16[256,2048]{1,0:T(8,128)(2,1)} collective-permute-done((bf16[256,2048]{1,0:T(8,128)(2,1)}, bf16[256,2048]{1,0:T(8,128)(2,1)}, u32[]{:S(2)}, u32[]{:S(2)}) %collective-permute-start.5) | collective-permute-done | bytes 1048608 | tf_op jit(solution)/shard_map/ppermute | solution.py:637
  132.1 15.7 %collective-permute-done.7 = bf16[256,2048]{1,0:T(8,128)(2,1)} collective-permute-done((bf16[256,2048]{1,0:T(8,128)(2,1)S(1)}, bf16[256,2048]{1,0:T(8,128)(2,1)}, u32[]{:S(2)}, u32[]{:S(2)}) %collective-permute-start.7) | collective-permute-done | bytes 1048608 | tf_op jit(solution)/shard_map/ppermute | solution.py:637
  150.5 19.2 %collective-permute-done.6 = bf16[256,2048]{1,0:T(8,128)(2,1)} collective-permute-done((bf16[256,2048]{1,0:T(8,128)(2,1)}, bf16[256,2048]{1,0:T(8,128)(2,1)}, u32[]{:S(2)}, u32[]{:S(2)}) %collective-permute-start.6) | collective-permute-done | bytes 1048608 | tf_op jit(solution)/shard_map/ppermute | solution.py:637
  172.8 15.7 %all-gather.6.cloned.1.call-done.gate_ref.up_ref.right_ref = bf16[2048,5632]{1,0:T(8,128)(2,1)} async-done(((bf16[128,5632]{1,0:T(8,128)(2,1)}), bf16[2048,5632]{1,0:T(8,128)(2,1)}) %all-gather.6.cloned.1.call-update) | async-done | bytes 23068688 | tf_op jit(solution)/shard_map/all_gather | solution.py:620
  188.6 22.7 %shard_map.487 = (f32[512,2816]{1,0:T(8,128)}, f32[512,2816]{1,0:T(8,128)}, bf16[512,2816]{1,0:T(8,128)(2,1)}) custom-call(bf16[512,2048]{1,0:T(8,128)(2,1)} %pad_maximum_fusion.2.hidden_ref.left_ref, bf16[2048,5632]{1,0:T(8,128)(2,1)} %all-gather.6.cloned.1.call-done.gate_ref.up_ref.right_ref, ...), custom_call_target="tpu_custom_call" | custom-call | flops 11811160064 | bytes 37486592 | tf_op jit(solution)/shard_map/pallas_call | solution.py:491
  211.2 8.9 %shard_map.489 = bf16[1024,2816]{1,0:T(8,128)(2,1)} custom-call(s32[1]{0:T(128)} %bitcast.11.half_ref, bf16[512,2048]{1,0:T(8,128)(2,1)} %pad_maximum_fusion.3.left_ref.cot_ref, bf16[1,512,2816]{2,1,0:T(8,128)(2,1)} %bitcast.32), custom_call_target="tpu_custom_call" | custom-call | flops 2952790016 | bytes 8650752 | tf_op jit(solution)/shard_map/pallas_call | solution.py:455
  220.3 10.9 %collective-permute-done.8.rest_0_ = bf16[1024,2816]{1,0:T(8,128)(2,1)} collective-permute-done((bf16[1024,2816]{1,0:T(8,128)(2,1)}, bf16[1024,2816]{1,0:T(8,128)(2,1)}, u32[]{:S(2)}, u32[]{:S(2)}) %collective-permute-start.8) | collective-permute-done | bytes 5767200 | tf_op jit(solution)/shard_map/ppermute | solution.py:628
  231.2 9.8 %shard_map.490 = bf16[1024,2816]{1,0:T(8,128)(2,1)} custom-call(s32[1]{0:T(128)} %bitcast.10.half_ref, bf16[512,2048]{1,0:T(8,128)(2,1)} %pad_maximum_fusion.3.left_ref.cot_ref, bf16[1,512,2816]{2,1,0:T(8,128)(2,1)} %bitcast.33, bf16[1024,2816]{1,0:T(8,128)(2,1)} %collective-permute-done.8.rest_0_), custom_call_target="tpu_custom_call" | custom-call | flops 2952790016 | bytes 14417920 | tf_op jit(solution)/shard_map/pallas_call | solution.py:455
  241.0 13.6 %all-gather.8.cloned.1.call-done.right_ref.down_ref = bf16[2048,2816]{1,0:T(8,128)(2,1)} async-done(((bf16[128,2816]{1,0:T(8,128)(2,1)}), bf16[2048,2816]{1,0:T(8,128)(2,1)}) %all-gather.8.cloned.1.call-update) | async-done | bytes 11534352 | tf_op jit(solution)/shard_map/all_gather | solution.py:620
  254.8 15.1 %shard_map.494.left_ref.right_ref = bf16[2,512,2816]{2,1,0:T(8,128)(2,1)} custom-call(bf16[512,2048]{1,0:T(8,128)(2,1)} %pad_maximum_fusion.3.left_ref.cot_ref, bf16[2048,2816]{1,0:T(8,128)(2,1)} %all-gather.8.cloned.1.call-done.right_ref.down_ref, f32[512,2816]{1,0:T(8,128)} %get-tuple-element.64.gate_ref, f32[512,2816]{1,0:T(8,128)} %get-tuple-element.65.up_ref), custom_call_target="tpu_custom_call" | custom-call | flops 5905580032 | bytes 28835840 | tf_op jit(solution)/shard_map/pallas_call | solution.py:523
  269.9 12.5 %shard_map.496 = bf16[256,2048]{1,0:T(8,128)(2,1)} custom-call(bf16[2,512,2816]{2,1,0:T(8,128)(2,1)} %shard_map.494.left_ref.right_ref, bf16[2048,5632]{1,0:T(8,128)(2,1)} %all-gather.6.cloned.1.call-done.gate_ref.up_ref.right_ref), custom_call_target="tpu_custom_call" | custom-call | flops 5905580032 | bytes 24117248 | tf_op jit(solution)/shard_map/pallas_call | solution.py:412
  283.9 12.8 %shard_map.495 = f32[256,2048]{1,0:T(8,128)} custom-call(bf16[2,512,2816]{2,1,0:T(8,128)(2,1)} %shard_map.494.left_ref.right_ref, bf16[2048,5632]{1,0:T(8,128)(2,1)} %all-gather.6.cloned.1.call-done.gate_ref.up_ref.right_ref), custom_call_target="tpu_custom_call" | custom-call | flops 5905580032 | bytes 25165824 | tf_op jit(solution)/shard_map/pallas_call | solution.py:412
  296.7 11.3 %collective-permute-done.10 = bf16[256,2048]{1,0:T(8,128)(2,1)S(1)} collective-permute-done((bf16[256,2048]{1,0:T(8,128)(2,1)}, bf16[256,2048]{1,0:T(8,128)(2,1)S(1)}, u32[]{:S(2)}, u32[]{:S(2)}) %collective-permute-start.10) | collective-permute-done | bytes 1048608 | tf_op jit(solution)/shard_map/ppermute | solution.py:637
  316.9 22.3 %collective-permute-done.11 = bf16[256,2048]{1,0:T(8,128)(2,1)S(1)} collective-permute-done((bf16[256,2048]{1,0:T(8,128)(2,1)S(1)}, bf16[256,2048]{1,0:T(8,128)(2,1)S(1)}, u32[]{:S(2)}, u32[]{:S(2)}) %collective-permute-start.11) | collective-permute-done | bytes 1048608 | tf_op jit(solution)/shard_map/ppermute | solution.py:637
  347.6 16.9 %shard_map.498 = bf16[512,1280]{1,0:T(8,128)(2,1)} custom-call(s32[1]{0:T(128)} %bitcast.at_ref, bf16[512,1024]{1,0:T(8,128)(2,1)} %shard_map.497.grad_ref, bf16[512,1024]{1,0:T(8,128)(2,1)} %get-tuple-element.66.query_ref, bf16[2,2,512,128]{3,2,1,0:T(8,128)(2,1)} %get-tuple-element.67.side_ref, bf16[512,128]{1,0:T(8,128)(2,1)} %get-tuple-element.68.key_ref, ...), custom_call_target="tpu_custom_call" | custom-call | flops 2684354560 | bytes 4194304 | tf_op jit(solution)/shard_map/pallas_call | solution.py:320
  377.1 13.6 %shard_map.507 = bf16[1024,5632]{1,0:T(8,128)(2,1)} custom-call(s32[1]{0:T(128)} %bitcast.11.half_ref, bf16[512,2048]{1,0:T(8,128)(2,1)} %pad_maximum_fusion.2.hidden_ref.left_ref, bf16[2,512,2816]{2,1,0:T(8,128)(2,1)} %shard_map.494.left_ref.right_ref), custom_call_target="tpu_custom_call" | custom-call | flops 5905580032 | bytes 17301504 | tf_op jit(solution)/shard_map/pallas_call | solution.py:455
  408.7 15.6 %shard_map.508 = bf16[1024,5632]{1,0:T(8,128)(2,1)} custom-call(s32[1]{0:T(128)} %bitcast.10.half_ref, bf16[512,2048]{1,0:T(8,128)(2,1)} %pad_maximum_fusion.2.hidden_ref.left_ref, bf16[2,512,2816]{2,1,0:T(8,128)(2,1)} %shard_map.494.left_ref.right_ref, bf16[1024,5632]{1,0:T(8,128)(2,1)} %collective-permute-done.20.rest_0_), custom_call_target="tpu_custom_call" | custom-call | flops 5905580032 | bytes 28835840 | tf_op jit(solution)/shard_map/pallas_call | solution.py:455
  439.6 16.9 %collective-permute-done.12 = bf16[256,2048]{1,0:T(8,128)(2,1)S(1)} collective-permute-done((bf16[256,2048]{1,0:T(8,128)(2,1)}, bf16[256,2048]{1,0:T(8,128)(2,1)S(1)}, u32[]{:S(2)}, u32[]{:S(2)}) %collective-permute-start.12) | collective-permute-done | bytes 1048608 | tf_op jit(solution)/shard_map/ppermute | solution.py:637
  469.1 9.2 %shard_map.491 = f32[256,2048]{1,0:T(8,128)} custom-call(bf16[1,512,2816]{2,1,0:T(8,128)(2,1)} %bitcast.35, bf16[2048,2816]{1,0:T(8,128)(2,1)} %all-gather.8.cloned.1.call-done.right_ref.down_ref), custom_call_target="tpu_custom_call" | custom-call | flops 2952790016 | bytes 13631488 | tf_op jit(solution)/shard_map/pallas_call | solution.py:412
  479.6 13.8 %collective-permute-done.9 = bf16[256,2048]{1,0:T(8,128)(2,1)} collective-permute-done((bf16[256,2048]{1,0:T(8,128)(2,1)}, bf16[256,2048]{1,0:T(8,128)(2,1)}, u32[]{:S(2)}, u32[]{:S(2)}) %collective-permute-start.9) | collective-permute-done | bytes 1048608 | tf_op jit(solution)/shard_map/ppermute | solution.py:637
  527.7 55.0 %reduce-scatter.6.cloned.1.call-done.gradient_ref = bf16[128,5632]{1,0:T(8,128)(2,1)} async-done(((bf16[1024,5632]{1,0:T(8,128)(2,1)}), bf16[128,5632]{1,0:T(8,128)(2,1)}) %reduce-scatter.6.cloned.1.call-update) | async-done | bytes 1441808 | tf_op jit(solution)/shard_map/reduce_scatter | solution.py:623
  582.7 11.7 %shard_map.509 = (f32[128,2,2816]{2,1,0:T(2,128)}, f32[128,2,2816]{2,1,0:T(2,128)}, f32[128,2,2816]{2,1,0:T(2,128)}, f32[128,2,2816]{2,1,0:T(2,128)}) custom-call(bf16[128,5632]{1,0:T(8,128)(2,1)} %reduce-scatter.6.cloned.1.call-done.gradient_ref, f32[128,2,2816]{2,1,0:T(2,128)} %refs_0_.6, f32[128,2,2816]{2,1,0:T(2,128)} %refs_1_.6, f32[128,2,2816]{2,1,0:T(2,128)} %refs_2_.6), custom_call_target="tpu_custom_call" | custom-call | flops 14417920 | bytes 20185088 | tf_op jit(solution)/shard_map/pallas_call | solution.py:602
  (144 shorter events, 198.0 us)
Async XLA Ops:
  7.2 60.5 %all-gather.4.cloned.1.call-start = ((), (), s32[]{:S(2)}) async-start(), calls=%async_computation.3 | async-start | bytes 10027008 | tf_op jit(solution)/shard_map/all_gather | solution.py:620
  9.5 179.0 %all-gather.6.cloned.1.call-start = ((), (), s32[]{:S(2)}) async-start(), calls=%async_computation.4 | async-start | bytes 24510464 | tf_op jit(solution)/shard_map/all_gather | solution.py:620
  13.7 240.8 %all-gather.8.cloned.1.call-start = ((), (), s32[]{:S(2)}) async-start(), calls=%async_computation.5 | async-start | bytes 12255232 | tf_op jit(solution)/shard_map/all_gather | solution.py:620
  15.3 501.8 %reduce-scatter.8.cloned.1.call-start = ((), (), s32[]{:S(2)}) async-start(), calls=%async_computation.8 | async-start | bytes 6488064 | tf_op jit(solution)/shard_map/reduce_scatter | solution.py:623
  16.7 4.4 collective-permute-start
  29.5 4.9 collective-permute-start.3
  34.7 23.5 %collective-permute-start.4 = (bf16[256,2048]{1,0:T(8,128)(2,1)S(1)}, bf16[256,2048]{1,0:T(8,128)(2,1)}, u32[]{:S(2)}, u32[]{:S(2)}) collective-permute-start(bf16[256,2048]{1,0:T(8,128)(2,1)S(1)} %multiply_convert_fusion.1), channel_id=1, source_target_pairs={{0,1},{1,0},{2,3},{3,2},{4,5},{5,4},{6,7},{7,6},{8,9},{9,8},{10,11... | collective-permute-start | bytes 3145736 | tf_op jit(solution)/shard_map/ppermute | solution.py:637
  98.9 26.3 %collective-permute-start.5 = (bf16[256,2048]{1,0:T(8,128)(2,1)}, bf16[256,2048]{1,0:T(8,128)(2,1)}, u32[]{:S(2)}, u32[]{:S(2)}) collective-permute-start(bf16[256,2048]{1,0:T(8,128)(2,1)} %shard_map.486), channel_id=1, source_target_pairs={{0,1},{1,0},{2,3},{3,2},{4,5},{5,4},{6,7},{7,6},{8,9},{9,8},{10,11... | collective-permute-start | bytes 3145736 | tf_op jit(solution)/shard_map/ppermute | solution.py:637
  106.3 41.4 %collective-permute-start.7 = (bf16[256,2048]{1,0:T(8,128)(2,1)S(1)}, bf16[256,2048]{1,0:T(8,128)(2,1)}, u32[]{:S(2)}, u32[]{:S(2)}) collective-permute-start(bf16[256,2048]{1,0:T(8,128)(2,1)S(1)} %convert_element_type.56), channel_id=1, source_target_pairs={{0,1},{1,0},{2,3},{3,2},{4,5},{5,4},{6,7},{7,6},{8,9},{9,8},{10,11... | collective-permute-start | bytes 3145736 | tf_op jit(solution)/shard_map/ppermute | solution.py:637
  130.3 39.4 %collective-permute-start.6 = (bf16[256,2048]{1,0:T(8,128)(2,1)}, bf16[256,2048]{1,0:T(8,128)(2,1)}, u32[]{:S(2)}, u32[]{:S(2)}) collective-permute-start(bf16[256,2048]{1,0:T(8,128)(2,1)} %multiply_convert_fusion), channel_id=1, source_target_pairs={{0,1},{1,0},{2,3},{3,2},{4,5},{5,4},{6,7},{7,6},{8,9},{9,8},{10,11... | collective-permute-start | bytes 3145736 | tf_op jit(solution)/shard_map/ppermute | solution.py:637
  220.1 11.0 %collective-permute-start.8 = (bf16[1024,2816]{1,0:T(8,128)(2,1)}, bf16[1024,2816]{1,0:T(8,128)(2,1)}, u32[]{:S(2)}, u32[]{:S(2)}) collective-permute-start(bf16[1024,2816]{1,0:T(8,128)(2,1)} %shard_map.489), channel_id=1, source_target_pairs={{0,2},{2,0},{4,6},{6,4},{8,10},{10,8},{12,14},{14,12},{16,18},{18,... | collective-permute-start | bytes 17301512 | tf_op jit(solution)/shard_map/ppermute | solution.py:628
  254.6 268.4 %reduce-scatter.4.cloned.1.call-start = ((), (), s32[]{:S(2)}) async-start(), calls=%async_computation.6 | async-start | bytes 5308416 | tf_op jit(solution)/shard_map/reduce_scatter | solution.py:623
  282.4 25.5 %collective-permute-start.10 = (bf16[256,2048]{1,0:T(8,128)(2,1)}, bf16[256,2048]{1,0:T(8,128)(2,1)S(1)}, u32[]{:S(2)}, u32[]{:S(2)}) collective-permute-start(bf16[256,2048]{1,0:T(8,128)(2,1)} %shard_map.496), channel_id=1, source_target_pairs={{0,1},{1,0},{2,3},{3,2},{4,5},{5,4},{6,7},{7,6},{8,9},{9,8},{10,11... | collective-permute-start | bytes 3145736 | tf_op jit(solution)/shard_map/ppermute | solution.py:637
  314.7 24.6 %collective-permute-start.11 = (bf16[256,2048]{1,0:T(8,128)(2,1)S(1)}, bf16[256,2048]{1,0:T(8,128)(2,1)S(1)}, u32[]{:S(2)}, u32[]{:S(2)}) collective-permute-start(bf16[256,2048]{1,0:T(8,128)(2,1)S(1)} %get-tuple-element.104), channel_id=1, source_target_pairs={{0,1},{1,0},{2,3},{3,2},{4,5},{5,4},{6,7},{7,6},{8,9},{9,8},{10,11... | collective-permute-start | bytes 3145736 | tf_op jit(solution)/shard_map/ppermute | solution.py:637
  370.8 26.0 %collective-permute-start.18 = (bf16[1024,1280]{1,0:T(8,128)(2,1)}, bf16[1024,1280]{1,0:T(8,128)(2,1)}, u32[]{:S(2)}, u32[]{:S(2)}) collective-permute-start(bf16[1024,1280]{1,0:T(8,128)(2,1)} %shard_map.502), channel_id=1, source_target_pairs={{0,2},{2,0},{4,6},{6,4},{8,10},{10,8},{12,14},{14,12},{16,18},{18,... | collective-permute-start | bytes 7864328 | tf_op jit(solution)/shard_map/ppermute | solution.py:628
  376.6 14.1 %collective-permute-start.19 = (bf16[1024,1024]{1,0:T(8,128)(2,1)}, bf16[1024,1024]{1,0:T(8,128)(2,1)}, u32[]{:S(2)}, u32[]{:S(2)}) collective-permute-start(bf16[1024,1024]{1,0:T(8,128)(2,1)} %shard_map.504), channel_id=1, source_target_pairs={{0,2},{2,0},{4,6},{6,4},{8,10},{10,8},{12,14},{14,12},{16,18},{18,... | collective-permute-start | bytes 6291464 | tf_op jit(solution)/shard_map/ppermute | solution.py:628
  390.7 18.1 %collective-permute-start.20 = (bf16[1024,5632]{1,0:T(8,128)(2,1)}, bf16[1024,5632]{1,0:T(8,128)(2,1)}, u32[]{:S(2)}, u32[]{:S(2)}) collective-permute-start(bf16[1024,5632]{1,0:T(8,128)(2,1)} %shard_map.507), channel_id=1, source_target_pairs={{0,2},{2,0},{4,6},{6,4},{8,10},{10,8},{12,14},{14,12},{16,18},{18,... | collective-permute-start | bytes 34603016 | tf_op jit(solution)/shard_map/ppermute | solution.py:628
  408.5 174.2 %reduce-scatter.6.cloned.1.call-start = ((), (), s32[]{:S(2)}) async-start(), calls=%async_computation.7 | async-start | bytes 12976128 | tf_op jit(solution)/shard_map/reduce_scatter | solution.py:623
  430.7 25.8 %collective-permute-start.12 = (bf16[256,2048]{1,0:T(8,128)(2,1)}, bf16[256,2048]{1,0:T(8,128)(2,1)S(1)}, u32[]{:S(2)}, u32[]{:S(2)}) collective-permute-start(bf16[256,2048]{1,0:T(8,128)(2,1)} %shard_map.500), channel_id=1, source_target_pairs={{0,1},{1,0},{2,3},{3,2},{4,5},{5,4},{6,7},{7,6},{8,9},{9,8},{10,11... | collective-permute-start | bytes 3145736 | tf_op jit(solution)/shard_map/ppermute | solution.py:637
  458.9 10.1 %collective-permute-start.13 = (f32[2,2048]{1,0:T(2,128)S(1)}, f32[2,2048]{1,0:T(2,128)S(1)}, u32[]{:S(2)}, u32[]{:S(2)}) collective-permute-start(f32[2,2048]{1,0:T(2,128)S(1)} %pad_maximum_fusion.6), channel_id=1, source_target_pairs={{0,1},{1,0},{2,3},{3,2},{4,5},{5,4},{6,7},{7,6},{8,9},{9,8},{10,11... | collective-permute-start | bytes 49160 | tf_op jit(solution)/shard_map/ppermute | solution.py:637
  468.5 24.8 %collective-permute-start.9 = (bf16[256,2048]{1,0:T(8,128)(2,1)}, bf16[256,2048]{1,0:T(8,128)(2,1)}, u32[]{:S(2)}, u32[]{:S(2)}) collective-permute-start(bf16[256,2048]{1,0:T(8,128)(2,1)} %shard_map.492), channel_id=1, source_target_pairs={{0,1},{1,0},{2,3},{3,2},{4,5},{5,4},{6,7},{7,6},{8,9},{9,8},{10,11... | collective-permute-start | bytes 3145736 | tf_op jit(solution)/shard_map/ppermute | solution.py:637
  469.0 9.3 %collective-permute-start.14 = (f32[2,2048]{1,0:T(2,128)S(1)}, f32[2,2048]{1,0:T(2,128)S(1)}, u32[]{:S(2)}, u32[]{:S(2)}) collective-permute-start(f32[2,2048]{1,0:T(2,128)S(1)} %fusion.6), channel_id=1, source_target_pairs={{0,2},{2,0},{4,6},{6,4},{8,10},{10,8},{12,14},{14,12},{16,18},{18,... | collective-permute-start | bytes 49160 | tf_op jit(solution)/shard_map/ppermute | solution.py:733
  478.3 23.4 %collective-permute-start.15 = (f32[2,2048]{1,0:T(2,128)S(1)}, f32[2,2048]{1,0:T(2,128)S(1)}, u32[]{:S(2)}, u32[]{:S(2)}) collective-permute-start(f32[2,2048]{1,0:T(2,128)S(1)} %fusion.11), channel_id=1, source_target_pairs={{0,4},{2,6},{4,0},{6,2},{8,12},{10,14},{12,8},{14,10},{16,20},{18,... | collective-permute-start | bytes 49160 | tf_op jit(solution)/shard_map/ppermute | solution.py:733
  506.0 10.5 %collective-permute-start.17 = (f32[2,2048]{1,0:T(2,128)S(1)}, f32[2,2048]{1,0:T(2,128)S(1)}, u32[]{:S(2)}, u32[]{:S(2)}) collective-permute-start(f32[2,2048]{1,0:T(2,128)S(1)} %add.130), channel_id=1, source_target_pairs={{0,16},{2,18},{4,20},{6,22},{8,24},{10,26},{12,28},{14,30},{16,0},... | collective-permute-start | bytes 49160 | tf_op jit(solution)/shard_map/ppermute | solution.py:733
  (17 other events, 97.2 us)
Sparse Core Ops, SparseCore 0:
  10.2 57.5 all-gather.3
  69.9 118.6 all-gather.5
  190.2 64.3 all-gather.7
  256.7 63.2 reduce-scatter.7
  408.6 53.4 reduce-scatter.3
  464.2 118.4 reduce-scatter.5

commit v2 on v1

--- a/solution.py
+++ b/solution.py
@@ -560,33 +560,43 @@
                 begin += ref.shape[-1]
 
     shape = jax.ShapeDtypeStruct((rows, wide), jnp.bfloat16)
+    blocks = 4
+
+    def spec(array):
+        inner = array.shape[1:]
+        return pl.BlockSpec((rows // blocks,) + inner, lambda i: (i,) + (0,) * len(inner))
+
     return pl.pallas_call(
         body,
-        in_specs=[pl.BlockSpec(memory_space=pltpu.VMEM)] * len(weights),
-        out_specs=pl.BlockSpec(memory_space=pltpu.VMEM),
+        grid=(blocks,),
+        in_specs=[spec(weight) for weight in weights],
+        out_specs=spec(shape),
         out_shape=shape,
         cost_estimate=cost_of(shape.size, shape, *weights),
     )(*weights)
 
 
-def adam_update(gradient, parameters, firsts, seconds, chunk):
+def adam_update(gradient, parameters, firsts, seconds, chunk, resident):
     rows = gradient.shape[0]
     chunk = min(rows, chunk)
     count = len(parameters)
 
     def body(gradient_ref, *refs):
         old, new = refs[: 3 * count], refs[3 * count :]
+        rows_at = pl.ds(pl.multiple_of(pl.program_id(0) * chunk, chunk), chunk)
         begin = 0
         for at in range(count):
             shape = old[3 * at].shape
             middle = range(shape[1]) if len(shape) == 3 else (None,)
             for part in middle:
                 wide = shape[-1]
-                where = (slice(None), slice(None)) if part is None else (slice(None), part, slice(None))
+                middles = () if part is None else (part,)
+                where = (slice(None), *middles, slice(None))
+                source = (rows_at, *middles, slice(None)) if resident else where
                 grads = gradient_ref[:, begin : begin + wide].astype(jnp.float32)
                 begin += wide
                 results = adam_step(
-                    old[3 * at][where], grads, old[3 * at + 1][where], old[3 * at + 2][where]
+                    old[3 * at][source], grads, old[3 * at + 1][source], old[3 * at + 2][source]
                 )
                 new[4 * at][where] = grads
                 for index, result in enumerate(results):
@@ -598,11 +608,16 @@
         )
 
     inputs = [array for group in zip(parameters, firsts, seconds) for array in group]
+    if resident:
+        inputs = [pltpu.with_memory_space_constraint(array, pltpu.VMEM) for array in inputs]
     outputs = [array for array in parameters for _ in range(4)]
     results = pl.pallas_call(
         body,
         grid=(rows // chunk,),
-        in_specs=[spec(gradient)] + [spec(array) for array in inputs],
+        in_specs=[spec(gradient)]
+        + [
+            pl.BlockSpec(memory_space=pltpu.VMEM) if resident else spec(array) for array in inputs
+        ],
         out_specs=[spec(array) for array in outputs],
         out_shape=[jax.ShapeDtypeStruct(array.shape, jnp.float32) for array in outputs],
         cost_estimate=cost_of(20 * gradient.size, *inputs, *outputs),
@@ -693,9 +708,7 @@
         cot_rows = both(cot_own.astype(bf16))
 
         qkv = times(hidden_one, attn_all, 0, qkv_wide, f32)
-        attn_cat, *saved = attend(
-            tensor_at, qkv, cosine_table, sine_table, segments, heads_wide
-        )
+        attn_cat, *saved = attend(tensor_at, qkv, cosine_table, sine_table, segments, heads_wide)
 
         residual = block_rows + summed(attn_cat, attn_all, qkv_wide)
         normed_two, inverse_two = norm_parts(residual)
@@ -739,20 +752,21 @@
         count = len(moments) // 2
         firsts, seconds = moments[:count], moments[count:]
 
-        def update(gradient, parameters, places, chunk):
+        def update(gradient, parameters, places, chunk, resident=False):
             results = adam_update(
                 gradient,
                 parameters,
                 [firsts[at] for at in places],
                 [seconds[at] for at in places],
                 chunk,
+                resident,
             )
             return dict(zip(places, results))
 
         attn_parameters = (query_weight, key_value_weight, out_weight)
         results = update(down_sum, (down_weight,), (6,), 32)
         results |= update(gate_up_sum, (gate_up_weight,), (5,), 16)
-        results |= update(attn_sum, attn_parameters, (1, 2, 3), 64)
+        results |= update(attn_sum, attn_parameters, (1, 2, 3), 32, True)
         for at, parameter, gradient in (
             (0, attn_gain, attn_gain_sum),
             (4, feed_gain, feed_gain_sum),

time: 603 us -> 604 us (level)
  transfers between devices with their start and end apart: 27 -> 27, of which waited for: 16 -> 17; matrix products, arithmetic and copies ran while one was open for 9% -> 9% of each run, Pallas kernels for 42% -> 42%
where the time goes in v2:
time: 604 us; the launch traced here: 602 us
  Pallas kernels  268 us (44%)
  waiting for transfers between devices  236 us (39%)
  other arithmetic  47.6 us (8%)
  starting transfers between devices  26.7 us (4%)
  between operations  15.2 us (3%)
  local copies, waits for them, and re-layouts  8 us (1%)
    ppermute x9, waiting for transfers between devices, swap(): return lax.ppermute(values, 'tensor', [(0, 1), (1, 0)])  128 us
    pallas_call x8, Pallas kernels, turned_times(): pl.pallas_call(body, grid_spec=pltpu.PrefetchScalarGridSpec(num_scalar_pr...  72.8 us
    pallas_call x8, Pallas kernels, times_turned(): pl.pallas_call(body, grid=(count // tile,), in_specs=[pl.BlockSpec((parts...  68.2 us
    reduce_scatter x3, waiting for transfers between devices, scatter(): lax.psum_scatter(values, 'dp', scatter_dimension=0, tiled=True, axis_inde...  55 us
    all_gather x3, waiting for transfers between devices, gather(): lax.all_gather(values, 'dp', axis=0, tiled=True, axis_index_groups=[order])  35.4 us
    pallas_call x1, Pallas kernels, feed_forward(): pl.pallas_call(body, grid=(wide // tile,), in_specs=[pl.BlockSpec((rows,...  22.7 us
    pallas_call x3, Pallas kernels, adam_update(): pl.pallas_call(body, grid=(rows // chunk,), in_specs=[spec(gradient)] + [...  22.2 us
    pallas_call x1, Pallas kernels, attend_back(): pl.pallas_call(attend_back_body, in_specs=whole_specs(12), out_specs=pl.B...  16.9 us
  transfers between devices with their start and end apart: 27, of which 17 were waited for; matrix products, arithmetic and copies ran while one was open for 9% of the time, Pallas kernels for 42%

profile of v2, /device:TPU:0, one launch (start us, length us, event | category | flops | bytes accessed | tf_op | source)
XLA Modules:
  0.0 602.0 jit_solution(12123382793705720688)
XLA Ops:
  43.1 16.5 %collective-permute-done.4 = bf16[256,2048]{1,0:T(8,128)(2,1)} collective-permute-done((bf16[256,2048]{1,0:T(8,128)(2,1)S(1)}, bf16[256,2048]{1,0:T(8,128)(2,1)}, u32[]{:S(2)}, u32[]{:S(2)}) %collective-permute-start.4) | collective-permute-done | bytes 1048608 | tf_op jit(solution)/shard_map/ppermute | solution.py:652
  76.6 16.8 %shard_map.484 = (bf16[512,1024]{1,0:T(8,128)(2,1)}, bf16[512,1024]{1,0:T(8,128)(2,1)}, bf16[2,2,512,128]{3,2,1,0:T(8,128)(2,1)}, bf16[512,128]{1,0:T(8,128)(2,1...) custom-call(s32[1]{0:T(128)} %bitcast.at_ref, f32[512,1280]{1,0:T(8,128)} %shard_map.483.qkv_ref, ...), custom_call_target="tpu_custom_call" | custom-call | flops 1073741824 | bytes 5242880 | tf_op jit(solution)/shard_map/pallas_call | solution.py:303
  113.8 12.1 %collective-permute-done.5 = bf16[256,2048]{1,0:T(8,128)(2,1)} collective-permute-done((bf16[256,2048]{1,0:T(8,128)(2,1)}, bf16[256,2048]{1,0:T(8,128)(2,1)}, u32[]{:S(2)}, u32[]{:S(2)}) %collective-permute-start.5) | collective-permute-done | bytes 1048608 | tf_op jit(solution)/shard_map/ppermute | solution.py:652
  132.7 15.7 %collective-permute-done.7 = bf16[256,2048]{1,0:T(8,128)(2,1)} collective-permute-done((bf16[256,2048]{1,0:T(8,128)(2,1)S(1)}, bf16[256,2048]{1,0:T(8,128)(2,1)}, u32[]{:S(2)}, u32[]{:S(2)}) %collective-permute-start.7) | collective-permute-done | bytes 1048608 | tf_op jit(solution)/shard_map/ppermute | solution.py:652
  151.1 19.2 %collective-permute-done.6 = bf16[256,2048]{1,0:T(8,128)(2,1)} collective-permute-done((bf16[256,2048]{1,0:T(8,128)(2,1)}, bf16[256,2048]{1,0:T(8,128)(2,1)}, u32[]{:S(2)}, u32[]{:S(2)}) %collective-permute-start.6) | collective-permute-done | bytes 1048608 | tf_op jit(solution)/shard_map/ppermute | solution.py:652
  173.5 15.7 %all-gather.6.cloned.1.call-done.gate_ref.up_ref.right_ref = bf16[2048,5632]{1,0:T(8,128)(2,1)} async-done(((bf16[128,5632]{1,0:T(8,128)(2,1)}), bf16[2048,5632]{1,0:T(8,128)(2,1)}) %all-gather.6.cloned.1.call-update) | async-done | bytes 23068688 | tf_op jit(solution)/shard_map/all_gather | solution.py:635
  189.2 22.7 %shard_map.487 = (f32[512,2816]{1,0:T(8,128)}, f32[512,2816]{1,0:T(8,128)}, bf16[512,2816]{1,0:T(8,128)(2,1)}) custom-call(bf16[512,2048]{1,0:T(8,128)(2,1)} %pad_maximum_fusion.2.hidden_ref.left_ref, bf16[2048,5632]{1,0:T(8,128)(2,1)} %all-gather.6.cloned.1.call-done.gate_ref.up_ref.right_ref, ...), custom_call_target="tpu_custom_call" | custom-call | flops 11811160064 | bytes 37486592 | tf_op jit(solution)/shard_map/pallas_call | solution.py:491
  211.9 8.8 %shard_map.489 = bf16[1024,2816]{1,0:T(8,128)(2,1)} custom-call(s32[1]{0:T(128)} %bitcast.11.half_ref, bf16[512,2048]{1,0:T(8,128)(2,1)} %pad_maximum_fusion.3.left_ref.cot_ref, bf16[1,512,2816]{2,1,0:T(8,128)(2,1)} %bitcast.32), custom_call_target="tpu_custom_call" | custom-call | flops 2952790016 | bytes 8650752 | tf_op jit(solution)/shard_map/pallas_call | solution.py:455
  220.9 10.9 %collective-permute-done.8.rest_0_ = bf16[1024,2816]{1,0:T(8,128)(2,1)} collective-permute-done((bf16[1024,2816]{1,0:T(8,128)(2,1)}, bf16[1024,2816]{1,0:T(8,128)(2,1)}, u32[]{:S(2)}, u32[]{:S(2)}) %collective-permute-start.8) | collective-permute-done | bytes 5767200 | tf_op jit(solution)/shard_map/ppermute | solution.py:643
  231.8 9.7 %shard_map.490 = bf16[1024,2816]{1,0:T(8,128)(2,1)} custom-call(s32[1]{0:T(128)} %bitcast.10.half_ref, bf16[512,2048]{1,0:T(8,128)(2,1)} %pad_maximum_fusion.3.left_ref.cot_ref, bf16[1,512,2816]{2,1,0:T(8,128)(2,1)} %bitcast.33, bf16[1024,2816]{1,0:T(8,128)(2,1)} %collective-permute-done.8.rest_0_), custom_call_target="tpu_custom_call" | custom-call | flops 2952790016 | bytes 14417920 | tf_op jit(solution)/shard_map/pallas_call | solution.py:455
  241.5 13.6 %all-gather.8.cloned.1.call-done.right_ref.down_ref = bf16[2048,2816]{1,0:T(8,128)(2,1)} async-done(((bf16[128,2816]{1,0:T(8,128)(2,1)}), bf16[2048,2816]{1,0:T(8,128)(2,1)}) %all-gather.8.cloned.1.call-update) | async-done | bytes 11534352 | tf_op jit(solution)/shard_map/all_gather | solution.py:635
  255.4 15.1 %shard_map.494.left_ref.right_ref = bf16[2,512,2816]{2,1,0:T(8,128)(2,1)} custom-call(bf16[512,2048]{1,0:T(8,128)(2,1)} %pad_maximum_fusion.3.left_ref.cot_ref, bf16[2048,2816]{1,0:T(8,128)(2,1)} %all-gather.8.cloned.1.call-done.right_ref.down_ref, f32[512,2816]{1,0:T(8,128)} %get-tuple-element.64.gate_ref, f32[512,2816]{1,0:T(8,128)} %get-tuple-element.65.up_ref), custom_call_target="tpu_custom_call" | custom-call | flops 5905580032 | bytes 28835840 | tf_op jit(solution)/shard_map/pallas_call | solution.py:523
  270.6 12.5 %shard_map.496 = bf16[256,2048]{1,0:T(8,128)(2,1)} custom-call(bf16[2,512,2816]{2,1,0:T(8,128)(2,1)} %shard_map.494.left_ref.right_ref, bf16[2048,5632]{1,0:T(8,128)(2,1)} %all-gather.6.cloned.1.call-done.gate_ref.up_ref.right_ref), custom_call_target="tpu_custom_call" | custom-call | flops 5905580032 | bytes 24117248 | tf_op jit(solution)/shard_map/pallas_call | solution.py:412
  284.6 12.8 %shard_map.495 = f32[256,2048]{1,0:T(8,128)} custom-call(bf16[2,512,2816]{2,1,0:T(8,128)(2,1)} %shard_map.494.left_ref.right_ref, bf16[2048,5632]{1,0:T(8,128)(2,1)} %all-gather.6.cloned.1.call-done.gate_ref.up_ref.right_ref), custom_call_target="tpu_custom_call" | custom-call | flops 5905580032 | bytes 25165824 | tf_op jit(solution)/shard_map/pallas_call | solution.py:412
  297.3 11.3 %collective-permute-done.10 = bf16[256,2048]{1,0:T(8,128)(2,1)S(1)} collective-permute-done((bf16[256,2048]{1,0:T(8,128)(2,1)}, bf16[256,2048]{1,0:T(8,128)(2,1)S(1)}, u32[]{:S(2)}, u32[]{:S(2)}) %collective-permute-start.10) | collective-permute-done | bytes 1048608 | tf_op jit(solution)/shard_map/ppermute | solution.py:652
  317.6 22.3 %collective-permute-done.11 = bf16[256,2048]{1,0:T(8,128)(2,1)S(1)} collective-permute-done((bf16[256,2048]{1,0:T(8,128)(2,1)S(1)}, bf16[256,2048]{1,0:T(8,128)(2,1)S(1)}, u32[]{:S(2)}, u32[]{:S(2)}) %collective-permute-start.11) | collective-permute-done | bytes 1048608 | tf_op jit(solution)/shard_map/ppermute | solution.py:652
  348.3 16.9 %shard_map.498 = bf16[512,1280]{1,0:T(8,128)(2,1)} custom-call(s32[1]{0:T(128)} %bitcast.at_ref, bf16[512,1024]{1,0:T(8,128)(2,1)} %shard_map.497.grad_ref, bf16[512,1024]{1,0:T(8,128)(2,1)} %get-tuple-element.66.query_ref, bf16[2,2,512,128]{3,2,1,0:T(8,128)(2,1)} %get-tuple-element.67.side_ref, bf16[512,128]{1,0:T(8,128)(2,1)} %get-tuple-element.68.key_ref, ...), custom_call_target="tpu_custom_call" | custom-call | flops 2684354560 | bytes 4194304 | tf_op jit(solution)/shard_map/pallas_call | solution.py:320
  377.8 13.6 %shard_map.507 = bf16[1024,5632]{1,0:T(8,128)(2,1)} custom-call(s32[1]{0:T(128)} %bitcast.11.half_ref, bf16[512,2048]{1,0:T(8,128)(2,1)} %pad_maximum_fusion.2.hidden_ref.left_ref, bf16[2,512,2816]{2,1,0:T(8,128)(2,1)} %shard_map.494.left_ref.right_ref), custom_call_target="tpu_custom_call" | custom-call | flops 5905580032 | bytes 17301504 | tf_op jit(solution)/shard_map/pallas_call | solution.py:455
  409.5 15.6 %shard_map.508 = bf16[1024,5632]{1,0:T(8,128)(2,1)} custom-call(s32[1]{0:T(128)} %bitcast.10.half_ref, bf16[512,2048]{1,0:T(8,128)(2,1)} %pad_maximum_fusion.2.hidden_ref.left_ref, bf16[2,512,2816]{2,1,0:T(8,128)(2,1)} %shard_map.494.left_ref.right_ref, bf16[1024,5632]{1,0:T(8,128)(2,1)} %collective-permute-done.20.rest_0_), custom_call_target="tpu_custom_call" | custom-call | flops 5905580032 | bytes 28835840 | tf_op jit(solution)/shard_map/pallas_call | solution.py:455
  440.4 16.9 %collective-permute-done.12 = bf16[256,2048]{1,0:T(8,128)(2,1)S(1)} collective-permute-done((bf16[256,2048]{1,0:T(8,128)(2,1)}, bf16[256,2048]{1,0:T(8,128)(2,1)S(1)}, u32[]{:S(2)}, u32[]{:S(2)}) %collective-permute-start.12) | collective-permute-done | bytes 1048608 | tf_op jit(solution)/shard_map/ppermute | solution.py:652
  469.8 9.2 %shard_map.491 = f32[256,2048]{1,0:T(8,128)} custom-call(bf16[1,512,2816]{2,1,0:T(8,128)(2,1)} %bitcast.35, bf16[2048,2816]{1,0:T(8,128)(2,1)} %all-gather.8.cloned.1.call-done.right_ref.down_ref), custom_call_target="tpu_custom_call" | custom-call | flops 2952790016 | bytes 13631488 | tf_op jit(solution)/shard_map/pallas_call | solution.py:412
  480.2 13.9 %collective-permute-done.9 = bf16[256,2048]{1,0:T(8,128)(2,1)} collective-permute-done((bf16[256,2048]{1,0:T(8,128)(2,1)}, bf16[256,2048]{1,0:T(8,128)(2,1)}, u32[]{:S(2)}, u32[]{:S(2)}) %collective-permute-start.9) | collective-permute-done | bytes 1048608 | tf_op jit(solution)/shard_map/ppermute | solution.py:652
  528.5 54.9 %reduce-scatter.6.cloned.1.call-done.gradient_ref = bf16[128,5632]{1,0:T(8,128)(2,1)} async-done(((bf16[1024,5632]{1,0:T(8,128)(2,1)}), bf16[128,5632]{1,0:T(8,128)(2,1)}) %reduce-scatter.6.cloned.1.call-update) | async-done | bytes 1441808 | tf_op jit(solution)/shard_map/reduce_scatter | solution.py:638
  583.5 11.7 %shard_map.509 = (f32[128,2,2816]{2,1,0:T(2,128)}, f32[128,2,2816]{2,1,0:T(2,128)}, f32[128,2,2816]{2,1,0:T(2,128)}, f32[128,2,2816]{2,1,0:T(2,128)}) custom-call(bf16[128,5632]{1,0:T(8,128)(2,1)} %reduce-scatter.6.cloned.1.call-done.gradient_ref, f32[128,2,2816]{2,1,0:T(2,128)} %refs_0_.6, f32[128,2,2816]{2,1,0:T(2,128)} %refs_1_.6, f32[128,2,2816]{2,1,0:T(2,128)} %refs_2_.6), custom_call_target="tpu_custom_call" | custom-call | flops 14417920 | bytes 20185088 | tf_op jit(solution)/shard_map/pallas_call | solution.py:614
  (162 shorter events, 198.3 us)
Async XLA Ops:
  7.2 61.2 %all-gather.4.cloned.1.call-start = ((), (), s32[]{:S(2)}) async-start(), calls=%async_computation.3 | async-start | bytes 10027008 | tf_op jit(solution)/shard_map/all_gather | solution.py:635
  10.7 178.5 %all-gather.6.cloned.1.call-start = ((), (), s32[]{:S(2)}) async-start(), calls=%async_computation.4 | async-start | bytes 24510464 | tf_op jit(solution)/shard_map/all_gather | solution.py:635
  14.9 240.3 %all-gather.8.cloned.1.call-start = ((), (), s32[]{:S(2)}) async-start(), calls=%async_computation.5 | async-start | bytes 12255232 | tf_op jit(solution)/shard_map/all_gather | solution.py:635
  16.4 501.5 %reduce-scatter.8.cloned.1.call-start = ((), (), s32[]{:S(2)}) async-start(), calls=%async_computation.8 | async-start | bytes 6488064 | tf_op jit(solution)/shard_map/reduce_scatter | solution.py:638
  22.3 4.5 collective-permute-start.1
  30.8 4.9 collective-permute-start.3
  35.9 23.7 %collective-permute-start.4 = (bf16[256,2048]{1,0:T(8,128)(2,1)S(1)}, bf16[256,2048]{1,0:T(8,128)(2,1)}, u32[]{:S(2)}, u32[]{:S(2)}) collective-permute-start(bf16[256,2048]{1,0:T(8,128)(2,1)S(1)} %multiply_convert_fusion.1), channel_id=1, source_target_pairs={{0,1},{1,0},{2,3},{3,2},{4,5},{5,4},{6,7},{7,6},{8,9},{9,8},{10,11... | collective-permute-start | bytes 3145736 | tf_op jit(solution)/shard_map/ppermute | solution.py:652
  99.6 26.3 %collective-permute-start.5 = (bf16[256,2048]{1,0:T(8,128)(2,1)}, bf16[256,2048]{1,0:T(8,128)(2,1)}, u32[]{:S(2)}, u32[]{:S(2)}) collective-permute-start(bf16[256,2048]{1,0:T(8,128)(2,1)} %shard_map.486), channel_id=1, source_target_pairs={{0,1},{1,0},{2,3},{3,2},{4,5},{5,4},{6,7},{7,6},{8,9},{9,8},{10,11... | collective-permute-start | bytes 3145736 | tf_op jit(solution)/shard_map/ppermute | solution.py:652
  107.0 41.4 %collective-permute-start.7 = (bf16[256,2048]{1,0:T(8,128)(2,1)S(1)}, bf16[256,2048]{1,0:T(8,128)(2,1)}, u32[]{:S(2)}, u32[]{:S(2)}) collective-permute-start(bf16[256,2048]{1,0:T(8,128)(2,1)S(1)} %convert_element_type.56), channel_id=1, source_target_pairs={{0,1},{1,0},{2,3},{3,2},{4,5},{5,4},{6,7},{7,6},{8,9},{9,8},{10,11... | collective-permute-start | bytes 3145736 | tf_op jit(solution)/shard_map/ppermute | solution.py:652
  130.9 39.4 %collective-permute-start.6 = (bf16[256,2048]{1,0:T(8,128)(2,1)}, bf16[256,2048]{1,0:T(8,128)(2,1)}, u32[]{:S(2)}, u32[]{:S(2)}) collective-permute-start(bf16[256,2048]{1,0:T(8,128)(2,1)} %multiply_convert_fusion), channel_id=1, source_target_pairs={{0,1},{1,0},{2,3},{3,2},{4,5},{5,4},{6,7},{7,6},{8,9},{9,8},{10,11... | collective-permute-start | bytes 3145736 | tf_op jit(solution)/shard_map/ppermute | solution.py:652
  220.8 11.0 %collective-permute-start.8 = (bf16[1024,2816]{1,0:T(8,128)(2,1)}, bf16[1024,2816]{1,0:T(8,128)(2,1)}, u32[]{:S(2)}, u32[]{:S(2)}) collective-permute-start(bf16[1024,2816]{1,0:T(8,128)(2,1)} %shard_map.489), channel_id=1, source_target_pairs={{0,2},{2,0},{4,6},{6,4},{8,10},{10,8},{12,14},{14,12},{16,18},{18,... | collective-permute-start | bytes 17301512 | tf_op jit(solution)/shard_map/ppermute | solution.py:643
  255.2 268.8 %reduce-scatter.4.cloned.1.call-start = ((), (), s32[]{:S(2)}) async-start(), calls=%async_computation.6 | async-start | bytes 5308416 | tf_op jit(solution)/shard_map/reduce_scatter | solution.py:638
  283.1 25.6 %collective-permute-start.10 = (bf16[256,2048]{1,0:T(8,128)(2,1)}, bf16[256,2048]{1,0:T(8,128)(2,1)S(1)}, u32[]{:S(2)}, u32[]{:S(2)}) collective-permute-start(bf16[256,2048]{1,0:T(8,128)(2,1)} %shard_map.496), channel_id=1, source_target_pairs={{0,1},{1,0},{2,3},{3,2},{4,5},{5,4},{6,7},{7,6},{8,9},{9,8},{10,11... | collective-permute-start | bytes 3145736 | tf_op jit(solution)/shard_map/ppermute | solution.py:652
  315.4 24.6 %collective-permute-start.11 = (bf16[256,2048]{1,0:T(8,128)(2,1)S(1)}, bf16[256,2048]{1,0:T(8,128)(2,1)S(1)}, u32[]{:S(2)}, u32[]{:S(2)}) collective-permute-start(bf16[256,2048]{1,0:T(8,128)(2,1)S(1)} %get-tuple-element.104), channel_id=1, source_target_pairs={{0,1},{1,0},{2,3},{3,2},{4,5},{5,4},{6,7},{7,6},{8,9},{9,8},{10,11... | collective-permute-start | bytes 3145736 | tf_op jit(solution)/shard_map/ppermute | solution.py:652
  371.5 26.0 %collective-permute-start.18 = (bf16[1024,1280]{1,0:T(8,128)(2,1)}, bf16[1024,1280]{1,0:T(8,128)(2,1)}, u32[]{:S(2)}, u32[]{:S(2)}) collective-permute-start(bf16[1024,1280]{1,0:T(8,128)(2,1)} %shard_map.502), channel_id=1, source_target_pairs={{0,2},{2,0},{4,6},{6,4},{8,10},{10,8},{12,14},{14,12},{16,18},{18,... | collective-permute-start | bytes 7864328 | tf_op jit(solution)/shard_map/ppermute | solution.py:643
  377.3 14.1 %collective-permute-start.19 = (bf16[1024,1024]{1,0:T(8,128)(2,1)}, bf16[1024,1024]{1,0:T(8,128)(2,1)}, u32[]{:S(2)}, u32[]{:S(2)}) collective-permute-start(bf16[1024,1024]{1,0:T(8,128)(2,1)} %shard_map.504), channel_id=1, source_target_pairs={{0,2},{2,0},{4,6},{6,4},{8,10},{10,8},{12,14},{14,12},{16,18},{18,... | collective-permute-start | bytes 6291464 | tf_op jit(solution)/shard_map/ppermute | solution.py:643
  391.4 18.1 %collective-permute-start.20 = (bf16[1024,5632]{1,0:T(8,128)(2,1)}, bf16[1024,5632]{1,0:T(8,128)(2,1)}, u32[]{:S(2)}, u32[]{:S(2)}) collective-permute-start(bf16[1024,5632]{1,0:T(8,128)(2,1)} %shard_map.507), channel_id=1, source_target_pairs={{0,2},{2,0},{4,6},{6,4},{8,10},{10,8},{12,14},{14,12},{16,18},{18,... | collective-permute-start | bytes 34603016 | tf_op jit(solution)/shard_map/ppermute | solution.py:643
  409.2 174.3 %reduce-scatter.6.cloned.1.call-start = ((), (), s32[]{:S(2)}) async-start(), calls=%async_computation.7 | async-start | bytes 12976128 | tf_op jit(solution)/shard_map/reduce_scatter | solution.py:638
  431.5 25.8 %collective-permute-start.12 = (bf16[256,2048]{1,0:T(8,128)(2,1)}, bf16[256,2048]{1,0:T(8,128)(2,1)S(1)}, u32[]{:S(2)}, u32[]{:S(2)}) collective-permute-start(bf16[256,2048]{1,0:T(8,128)(2,1)} %shard_map.500), channel_id=1, source_target_pairs={{0,1},{1,0},{2,3},{3,2},{4,5},{5,4},{6,7},{7,6},{8,9},{9,8},{10,11... | collective-permute-start | bytes 3145736 | tf_op jit(solution)/shard_map/ppermute | solution.py:652
  459.6 10.1 %collective-permute-start.13 = (f32[2,2048]{1,0:T(2,128)S(1)}, f32[2,2048]{1,0:T(2,128)S(1)}, u32[]{:S(2)}, u32[]{:S(2)}) collective-permute-start(f32[2,2048]{1,0:T(2,128)S(1)} %pad_maximum_fusion.6), channel_id=1, source_target_pairs={{0,1},{1,0},{2,3},{3,2},{4,5},{5,4},{6,7},{7,6},{8,9},{9,8},{10,11... | collective-permute-start | bytes 49160 | tf_op jit(solution)/shard_map/ppermute | solution.py:652
  469.2 24.8 %collective-permute-start.9 = (bf16[256,2048]{1,0:T(8,128)(2,1)}, bf16[256,2048]{1,0:T(8,128)(2,1)}, u32[]{:S(2)}, u32[]{:S(2)}) collective-permute-start(bf16[256,2048]{1,0:T(8,128)(2,1)} %shard_map.492), channel_id=1, source_target_pairs={{0,1},{1,0},{2,3},{3,2},{4,5},{5,4},{6,7},{7,6},{8,9},{9,8},{10,11... | collective-permute-start | bytes 3145736 | tf_op jit(solution)/shard_map/ppermute | solution.py:652
  469.7 9.3 %collective-permute-start.14 = (f32[2,2048]{1,0:T(2,128)S(1)}, f32[2,2048]{1,0:T(2,128)S(1)}, u32[]{:S(2)}, u32[]{:S(2)}) collective-permute-start(f32[2,2048]{1,0:T(2,128)S(1)} %fusion.6), channel_id=1, source_target_pairs={{0,2},{2,0},{4,6},{6,4},{8,10},{10,8},{12,14},{14,12},{16,18},{18,... | collective-permute-start | bytes 49160 | tf_op jit(solution)/shard_map/ppermute | solution.py:746
  479.0 23.4 %collective-permute-start.15 = (f32[2,2048]{1,0:T(2,128)S(1)}, f32[2,2048]{1,0:T(2,128)S(1)}, u32[]{:S(2)}, u32[]{:S(2)}) collective-permute-start(f32[2,2048]{1,0:T(2,128)S(1)} %fusion.11), channel_id=1, source_target_pairs={{0,4},{2,6},{4,0},{6,2},{8,12},{10,14},{12,8},{14,10},{16,20},{18,... | collective-permute-start | bytes 49160 | tf_op jit(solution)/shard_map/ppermute | solution.py:746
  506.7 10.5 %collective-permute-start.17 = (f32[2,2048]{1,0:T(2,128)S(1)}, f32[2,2048]{1,0:T(2,128)S(1)}, u32[]{:S(2)}, u32[]{:S(2)}) collective-permute-start(f32[2,2048]{1,0:T(2,128)S(1)} %add.130), channel_id=1, source_target_pairs={{0,16},{2,18},{4,20},{6,22},{8,24},{10,26},{12,28},{14,30},{16,0},... | collective-permute-start | bytes 49160 | tf_op jit(solution)/shard_map/ppermute | solution.py:746
  (26 other events, 153.6 us)
Sparse Core Ops, SparseCore 0:
  10.8 57.5 all-gather.3
  70.6 118.6 all-gather.5
  190.8 64.3 all-gather.7
  257.3 63.2 reduce-scatter.7
  409.3 53.4 reduce-scatter.3
  465.0 118.4 reduce-scatter.5

commit v3 on v1

--- a/solution.py
+++ b/solution.py
@@ -627,6 +627,24 @@
     def swap_core(values):
         return lax.ppermute(values, "dp", [(i, i ^ 1) for i in range(dp_size)])
 
+    def halve_scatter(values):
+        place = jnp.asarray(inverse_order, jnp.int32)[lax.axis_index("dp")] % chips
+        rest = values.reshape(2, chips // 2, -1, values.shape[1]).astype(jnp.float32)
+
+        def halved(first, second, upper, mask):
+            keep, send = jnp.where(upper, second, first), jnp.where(upper, first, second)
+            pairs = [(ring[i], ring[i ^ mask]) for ring in rings for i in range(chips)]
+            received = lax.ppermute(send.astype(jnp.bfloat16), "dp", pairs)
+            return keep + received.astype(jnp.float32)
+
+        rest = halved(rest[0], rest[1], place >= chips // 2, chips - 1)
+        bit = 1
+        while bit < chips // 2:
+            rest = rest.reshape(rest.shape[0] // 2, 2, *rest.shape[1:])
+            rest = halved(rest[:, 0], rest[:, 1], place // bit % 2 == 1, bit)
+            bit *= 2
+        return rest[0].astype(jnp.bfloat16)
+
     def pair_grad(left, right):
         core = lax.axis_index("dp") % 2
         other = turned_times(left, 1 - core, right)
@@ -723,8 +741,14 @@
         input_grad = grad_residual + norm_back(grad_hidden_one, gain_one, normed_one, inverse_one)
         attn_gain_part = jnp.sum(grad_hidden_one * normed_one, axis=0)
 
-        parts = [rows_major(qkv_grad), rows_major(out_grad)]
+        parts = [rows_major(qkv_grad[:, :heads_wide]), rows_major(out_grad)]
         attn_sum = rows_major(scatter(jnp.concatenate(parts, axis=1)))
+        key_value_grad = qkv_grad[:, heads_wide:]
+        if chips & (chips - 1):
+            key_value_sum = scatter(key_value_grad)
+        else:
+            key_value_sum = halve_scatter(key_value_grad)
+
         gain_parts = jnp.stack([attn_gain_part, feed_gain_part])
         gain_parts = gain_parts + swap(gain_parts)
         step = 1
@@ -749,10 +773,11 @@
             )
             return dict(zip(places, results))
 
-        attn_parameters = (query_weight, key_value_weight, out_weight)
+        attn_parameters = (query_weight, out_weight)
         results = update(down_sum, (down_weight,), (6,), 32)
         results |= update(gate_up_sum, (gate_up_weight,), (5,), 16)
-        results |= update(attn_sum, attn_parameters, (1, 2, 3), 64)
+        results |= update(attn_sum, attn_parameters, (1, 3), 64)
+        results |= update(key_value_sum, (key_value_weight,), (2,), 64)
         for at, parameter, gradient in (
             (0, attn_gain, attn_gain_sum),
             (4, feed_gain, feed_gain_sum),

time: 603 us -> 596 us (0.988)
  waiting for transfers between devices: 236 us -> 221 us
    reduce_scatter x3, waiting for transfers between devices: 55 us -> 35.8 us  [scatter(): lax.psum_scatter(values, 'dp', scatter_dimension=0, tiled=True, axis_inde...]
    ppermute x0 -> x3, waiting for transfers between devices: none -> 17.3 us  [halved(): received = lax.ppermute(send.astype(jnp.bfloat16), 'dp', pairs)]
    ppermute x9, waiting for transfers between devices: 127 us -> 113 us  [swap(): return lax.ppermute(values, 'tensor', [(0, 1), (1, 0)])]
    pallas_call x3 -> x4, Pallas kernels: 22.3 us -> 23.8 us  [adam_update(): pl.pallas_call(body, grid=(rows // chunk,), in_specs=[spec(gradient)] + [...]
  transfers between devices with their start and end apart: 27 -> 30, of which waited for: 16 -> 20; matrix products, arithmetic and copies ran while one was open for 9% -> 9% of each run, Pallas kernels for 42% -> 43%
where the time goes in v3:
time: 596 us; the launch traced here: 594 us
  Pallas kernels  269 us (45%)
  waiting for transfers between devices  221 us (37%)
  other arithmetic  46.6 us (8%)
  starting transfers between devices  28.5 us (5%)
  between operations  17.2 us (3%)
  local copies, waits for them, and re-layouts  11 us (2%)
    ppermute x9, waiting for transfers between devices, swap(): return lax.ppermute(values, 'tensor', [(0, 1), (1, 0)])  113 us
    pallas_call x8, Pallas kernels, turned_times(): pl.pallas_call(body, grid_spec=pltpu.PrefetchScalarGridSpec(num_scalar_pr...  73.1 us
    pallas_call x8, Pallas kernels, times_turned(): pl.pallas_call(body, grid=(count // tile,), in_specs=[pl.BlockSpec((parts...  68 us
    all_gather x3, waiting for transfers between devices, gather(): lax.all_gather(values, 'dp', axis=0, tiled=True, axis_index_groups=[order])  36.1 us
    reduce_scatter x3, waiting for transfers between devices, scatter(): lax.psum_scatter(values, 'dp', scatter_dimension=0, tiled=True, axis_inde...  35.8 us
    pallas_call x4, Pallas kernels, adam_update(): pl.pallas_call(body, grid=(rows // chunk,), in_specs=[spec(gradient)] + [...  23.8 us
    pallas_call x1, Pallas kernels, feed_forward(): pl.pallas_call(body, grid=(wide // tile,), in_specs=[pl.BlockSpec((rows,...  22.7 us
    ppermute x3, waiting for transfers between devices, halved(): received = lax.ppermute(send.astype(jnp.bfloat16), 'dp', pairs)  17.3 us
  transfers between devices with their start and end apart: 30, of which 20 were waited for; matrix products, arithmetic and copies ran while one was open for 9% of the time, Pallas kernels for 43%

profile of v3, /device:TPU:0, one launch (start us, length us, event | category | flops | bytes accessed | tf_op | source)
XLA Modules:
  0.0 593.6 jit_solution(7894240697216357516)
XLA Ops:
  42.0 16.2 %collective-permute-done.4 = bf16[256,2048]{1,0:T(8,128)(2,1)} collective-permute-done((bf16[256,2048]{1,0:T(8,128)(2,1)S(1)}, bf16[256,2048]{1,0:T(8,128)(2,1)}, u32[]{:S(2)}, u32[]{:S(2)}) %collective-permute-start.4) | collective-permute-done | bytes 1048608 | tf_op jit(solution)/shard_map/ppermute | solution.py:655
  76.0 16.8 %shard_map.493 = (bf16[512,1024]{1,0:T(8,128)(2,1)}, bf16[512,1024]{1,0:T(8,128)(2,1)}, bf16[2,2,512,128]{3,2,1,0:T(8,128)(2,1)}, bf16[512,128]{1,0:T(8,128)(2,1...) custom-call(s32[1]{0:T(128)} %bitcast.at_ref, f32[512,1280]{1,0:T(8,128)} %shard_map.492.qkv_ref, ...), custom_call_target="tpu_custom_call" | custom-call | flops 1073741824 | bytes 5242880 | tf_op jit(solution)/shard_map/pallas_call | solution.py:303
  113.2 12.1 %collective-permute-done.5 = bf16[256,2048]{1,0:T(8,128)(2,1)} collective-permute-done((bf16[256,2048]{1,0:T(8,128)(2,1)}, bf16[256,2048]{1,0:T(8,128)(2,1)}, u32[]{:S(2)}, u32[]{:S(2)}) %collective-permute-start.5) | collective-permute-done | bytes 1048608 | tf_op jit(solution)/shard_map/ppermute | solution.py:655
  132.1 15.7 %collective-permute-done.7 = bf16[256,2048]{1,0:T(8,128)(2,1)} collective-permute-done((bf16[256,2048]{1,0:T(8,128)(2,1)S(1)}, bf16[256,2048]{1,0:T(8,128)(2,1)}, u32[]{:S(2)}, u32[]{:S(2)}) %collective-permute-start.7) | collective-permute-done | bytes 1048608 | tf_op jit(solution)/shard_map/ppermute | solution.py:655
  150.5 19.2 %collective-permute-done.6 = bf16[256,2048]{1,0:T(8,128)(2,1)} collective-permute-done((bf16[256,2048]{1,0:T(8,128)(2,1)}, bf16[256,2048]{1,0:T(8,128)(2,1)}, u32[]{:S(2)}, u32[]{:S(2)}) %collective-permute-start.6) | collective-permute-done | bytes 1048608 | tf_op jit(solution)/shard_map/ppermute | solution.py:655
  172.8 15.7 %all-gather.6.cloned.1.call-done.gate_ref.up_ref.right_ref = bf16[2048,5632]{1,0:T(8,128)(2,1)} async-done(((bf16[128,5632]{1,0:T(8,128)(2,1)}), bf16[2048,5632]{1,0:T(8,128)(2,1)}) %all-gather.6.cloned.1.call-update) | async-done | bytes 23068688 | tf_op jit(solution)/shard_map/all_gather | solution.py:620
  188.6 22.7 %shard_map.496 = (f32[512,2816]{1,0:T(8,128)}, f32[512,2816]{1,0:T(8,128)}, bf16[512,2816]{1,0:T(8,128)(2,1)}) custom-call(bf16[512,2048]{1,0:T(8,128)(2,1)} %pad_maximum_fusion.2.hidden_ref.left_ref, bf16[2048,5632]{1,0:T(8,128)(2,1)} %all-gather.6.cloned.1.call-done.gate_ref.up_ref.right_ref, ...), custom_call_target="tpu_custom_call" | custom-call | flops 11811160064 | bytes 37486592 | tf_op jit(solution)/shard_map/pallas_call | solution.py:491
  211.2 8.9 %shard_map.498 = bf16[1024,2816]{1,0:T(8,128)(2,1)} custom-call(s32[1]{0:T(128)} %bitcast.11.half_ref, bf16[512,2048]{1,0:T(8,128)(2,1)} %pad_maximum_fusion.3.left_ref.cot_ref, bf16[1,512,2816]{2,1,0:T(8,128)(2,1)} %bitcast.69), custom_call_target="tpu_custom_call" | custom-call | flops 2952790016 | bytes 8650752 | tf_op jit(solution)/shard_map/pallas_call | solution.py:455
  220.3 10.9 %collective-permute-done.8.rest_0_ = bf16[1024,2816]{1,0:T(8,128)(2,1)} collective-permute-done((bf16[1024,2816]{1,0:T(8,128)(2,1)}, bf16[1024,2816]{1,0:T(8,128)(2,1)}, u32[]{:S(2)}, u32[]{:S(2)}) %collective-permute-start.8) | collective-permute-done | bytes 5767200 | tf_op jit(solution)/shard_map/ppermute | solution.py:628
  231.2 9.8 %shard_map.499 = bf16[1024,2816]{1,0:T(8,128)(2,1)} custom-call(s32[1]{0:T(128)} %bitcast.10.half_ref, bf16[512,2048]{1,0:T(8,128)(2,1)} %pad_maximum_fusion.3.left_ref.cot_ref, bf16[1,512,2816]{2,1,0:T(8,128)(2,1)} %bitcast.70, bf16[1024,2816]{1,0:T(8,128)(2,1)} %collective-permute-done.8.rest_0_), custom_call_target="tpu_custom_call" | custom-call | flops 2952790016 | bytes 14417920 | tf_op jit(solution)/shard_map/pallas_call | solution.py:455
  241.0 13.5 %all-gather.8.cloned.1.call-done.right_ref.down_ref = bf16[2048,2816]{1,0:T(8,128)(2,1)} async-done(((bf16[128,2816]{1,0:T(8,128)(2,1)}), bf16[2048,2816]{1,0:T(8,128)(2,1)}) %all-gather.8.cloned.1.call-update) | async-done | bytes 11534352 | tf_op jit(solution)/shard_map/all_gather | solution.py:620
  254.8 15.1 %shard_map.503.left_ref.right_ref = bf16[2,512,2816]{2,1,0:T(8,128)(2,1)} custom-call(bf16[512,2048]{1,0:T(8,128)(2,1)} %pad_maximum_fusion.3.left_ref.cot_ref, bf16[2048,2816]{1,0:T(8,128)(2,1)} %all-gather.8.cloned.1.call-done.right_ref.down_ref, f32[512,2816]{1,0:T(8,128)} %get-tuple-element.64.gate_ref, f32[512,2816]{1,0:T(8,128)} %get-tuple-element.65.up_ref), custom_call_target="tpu_custom_call" | custom-call | flops 5905580032 | bytes 28835840 | tf_op jit(solution)/shard_map/pallas_call | solution.py:523
  269.9 12.5 %shard_map.505 = bf16[256,2048]{1,0:T(8,128)(2,1)} custom-call(bf16[2,512,2816]{2,1,0:T(8,128)(2,1)} %shard_map.503.left_ref.right_ref, bf16[2048,5632]{1,0:T(8,128)(2,1)} %all-gather.6.cloned.1.call-done.gate_ref.up_ref.right_ref), custom_call_target="tpu_custom_call" | custom-call | flops 5905580032 | bytes 24117248 | tf_op jit(solution)/shard_map/pallas_call | solution.py:412
  283.9 12.8 %shard_map.504 = f32[256,2048]{1,0:T(8,128)} custom-call(bf16[2,512,2816]{2,1,0:T(8,128)(2,1)} %shard_map.503.left_ref.right_ref, bf16[2048,5632]{1,0:T(8,128)(2,1)} %all-gather.6.cloned.1.call-done.gate_ref.up_ref.right_ref), custom_call_target="tpu_custom_call" | custom-call | flops 5905580032 | bytes 25165824 | tf_op jit(solution)/shard_map/pallas_call | solution.py:412
  296.7 11.3 %collective-permute-done.10 = bf16[256,2048]{1,0:T(8,128)(2,1)S(1)} collective-permute-done((bf16[256,2048]{1,0:T(8,128)(2,1)}, bf16[256,2048]{1,0:T(8,128)(2,1)S(1)}, u32[]{:S(2)}, u32[]{:S(2)}) %collective-permute-start.10) | collective-permute-done | bytes 1048608 | tf_op jit(solution)/shard_map/ppermute | solution.py:655
  317.3 13.6 %shard_map.517 = bf16[1024,5632]{1,0:T(8,128)(2,1)} custom-call(s32[1]{0:T(128)} %bitcast.11.half_ref, bf16[512,2048]{1,0:T(8,128)(2,1)} %pad_maximum_fusion.2.hidden_ref.left_ref, bf16[2,512,2816]{2,1,0:T(8,128)(2,1)} %shard_map.503.left_ref.right_ref), custom_call_target="tpu_custom_call" | custom-call | flops 5905580032 | bytes 17301504 | tf_op jit(solution)/shard_map/pallas_call | solution.py:455
  330.9 8.9 %collective-permute-done.11 = bf16[256,2048]{1,0:T(8,128)(2,1)S(1)} collective-permute-done((bf16[256,2048]{1,0:T(8,128)(2,1)}, bf16[256,2048]{1,0:T(8,128)(2,1)S(1)}, u32[]{:S(2)}, u32[]{:S(2)}) %collective-permute-start.11) | collective-permute-done | bytes 1048608 | tf_op jit(solution)/shard_map/ppermute | solution.py:655
  349.4 16.9 %shard_map.507 = bf16[512,1280]{1,0:T(8,128)(2,1)} custom-call(s32[1]{0:T(128)} %bitcast.at_ref, bf16[512,1024]{1,0:T(8,128)(2,1)} %shard_map.506.grad_ref, bf16[512,1024]{1,0:T(8,128)(2,1)} %get-tuple-element.66.query_ref, bf16[2,2,512,128]{3,2,1,0:T(8,128)(2,1)} %get-tuple-element.67.side_ref, bf16[512,128]{1,0:T(8,128)(2,1)} %get-tuple-element.68.key_ref, ...), custom_call_target="tpu_custom_call" | custom-call | flops 2684354560 | bytes 4194304 | tf_op jit(solution)/shard_map/pallas_call | solution.py:320
  400.9 15.6 %shard_map.518 = bf16[1024,5632]{1,0:T(8,128)(2,1)} custom-call(s32[1]{0:T(128)} %bitcast.10.half_ref, bf16[512,2048]{1,0:T(8,128)(2,1)} %pad_maximum_fusion.2.hidden_ref.left_ref, bf16[2,512,2816]{2,1,0:T(8,128)(2,1)} %shard_map.503.left_ref.right_ref, bf16[1024,5632]{1,0:T(8,128)(2,1)} %collective-permute-done.23.rest_0_), custom_call_target="tpu_custom_call" | custom-call | flops 5905580032 | bytes 28835840 | tf_op jit(solution)/shard_map/pallas_call | solution.py:455
  433.7 14.8 %collective-permute-done.12 = bf16[256,2048]{1,0:T(8,128)(2,1)S(1)} collective-permute-done((bf16[256,2048]{1,0:T(8,128)(2,1)}, bf16[256,2048]{1,0:T(8,128)(2,1)S(1)}, u32[]{:S(2)}, u32[]{:S(2)}) %collective-permute-start.12) | collective-permute-done | bytes 1048608 | tf_op jit(solution)/shard_map/ppermute | solution.py:655
  470.8 14.7 %collective-permute-done.9 = bf16[256,2048]{1,0:T(8,128)(2,1)} collective-permute-done((bf16[256,2048]{1,0:T(8,128)(2,1)}, bf16[256,2048]{1,0:T(8,128)(2,1)}, u32[]{:S(2)}, u32[]{:S(2)}) %collective-permute-start.9) | collective-permute-done | bytes 1048608 | tf_op jit(solution)/shard_map/ppermute | solution.py:655
  500.4 9.8 %collective-permute-done.20 = bf16[4,128,256]{2,1,0:T(8,128)(2,1)S(1)} collective-permute-done((bf16[4,128,256]{2,1,0:T(8,128)(2,1)S(1)}, bf16[4,128,256]{2,1,0:T(8,128)(2,1)S(1)}, u32[]{:S(2)}, u32[]{:S(2)}) %collective-permute-start.20) | collective-permute-done | bytes 262176 | tf_op jit(solution)/shard_map/ppermute | solution.py:637
  539.3 35.8 %reduce-scatter.6.cloned.1.call-done.gradient_ref = bf16[128,5632]{1,0:T(8,128)(2,1)} async-done(((bf16[1024,5632]{1,0:T(8,128)(2,1)}), bf16[128,5632]{1,0:T(8,128)(2,1)}) %reduce-scatter.6.cloned.1.call-update) | async-done | bytes 1441808 | tf_op jit(solution)/shard_map/reduce_scatter | solution.py:623
  575.1 11.7 %shard_map.519 = (f32[128,2,2816]{2,1,0:T(2,128)}, f32[128,2,2816]{2,1,0:T(2,128)}, f32[128,2,2816]{2,1,0:T(2,128)}, f32[128,2,2816]{2,1,0:T(2,128)}) custom-call(bf16[128,5632]{1,0:T(8,128)(2,1)} %reduce-scatter.6.cloned.1.call-done.gradient_ref, f32[128,2,2816]{2,1,0:T(2,128)} %refs_0_.8, f32[128,2,2816]{2,1,0:T(2,128)} %refs_1_.8, f32[128,2,2816]{2,1,0:T(2,128)} %refs_2_.8), custom_call_target="tpu_custom_call" | custom-call | flops 14417920 | bytes 20185088 | tf_op jit(solution)/shard_map/pallas_call | solution.py:602
  (171 shorter events, 221.4 us)
Async XLA Ops:
  7.2 60.5 %all-gather.4.cloned.1.call-start = ((), (), s32[]{:S(2)}) async-start(), calls=%async_computation.3 | async-start | bytes 10027008 | tf_op jit(solution)/shard_map/all_gather | solution.py:620
  9.5 179.0 %all-gather.6.cloned.1.call-start = ((), (), s32[]{:S(2)}) async-start(), calls=%async_computation.4 | async-start | bytes 24510464 | tf_op jit(solution)/shard_map/all_gather | solution.py:620
  13.7 240.8 %all-gather.8.cloned.1.call-start = ((), (), s32[]{:S(2)}) async-start(), calls=%async_computation.5 | async-start | bytes 12255232 | tf_op jit(solution)/shard_map/all_gather | solution.py:620
  15.3 514.2 %reduce-scatter.8.cloned.1.call-start = ((), (), s32[]{:S(2)}) async-start(), calls=%async_computation.8 | async-start | bytes 6488064 | tf_op jit(solution)/shard_map/reduce_scatter | solution.py:623
  34.7 23.5 %collective-permute-start.4 = (bf16[256,2048]{1,0:T(8,128)(2,1)S(1)}, bf16[256,2048]{1,0:T(8,128)(2,1)}, u32[]{:S(2)}, u32[]{:S(2)}) collective-permute-start(bf16[256,2048]{1,0:T(8,128)(2,1)S(1)} %multiply_convert_fusion.1), channel_id=1, source_target_pairs={{0,1},{1,0},{2,3},{3,2},{4,5},{5,4},{6,7},{7,6},{8,9},{9,8},{10,11... | collective-permute-start | bytes 3145736 | tf_op jit(solution)/shard_map/ppermute | solution.py:655
  98.9 26.3 %collective-permute-start.5 = (bf16[256,2048]{1,0:T(8,128)(2,1)}, bf16[256,2048]{1,0:T(8,128)(2,1)}, u32[]{:S(2)}, u32[]{:S(2)}) collective-permute-start(bf16[256,2048]{1,0:T(8,128)(2,1)} %shard_map.495), channel_id=1, source_target_pairs={{0,1},{1,0},{2,3},{3,2},{4,5},{5,4},{6,7},{7,6},{8,9},{9,8},{10,11... | collective-permute-start | bytes 3145736 | tf_op jit(solution)/shard_map/ppermute | solution.py:655
  106.3 41.4 %collective-permute-start.7 = (bf16[256,2048]{1,0:T(8,128)(2,1)S(1)}, bf16[256,2048]{1,0:T(8,128)(2,1)}, u32[]{:S(2)}, u32[]{:S(2)}) collective-permute-start(bf16[256,2048]{1,0:T(8,128)(2,1)S(1)} %convert_element_type.101), channel_id=1, source_target_pairs={{0,1},{1,0},{2,3},{3,2},{4,5},{5,4},{6,7},{7,6},{8,9},{9,8},{10,11... | collective-permute-start | bytes 3145736 | tf_op jit(solution)/shard_map/ppermute | solution.py:655
  130.3 39.4 %collective-permute-start.6 = (bf16[256,2048]{1,0:T(8,128)(2,1)}, bf16[256,2048]{1,0:T(8,128)(2,1)}, u32[]{:S(2)}, u32[]{:S(2)}) collective-permute-start(bf16[256,2048]{1,0:T(8,128)(2,1)} %multiply_convert_fusion), channel_id=1, source_target_pairs={{0,1},{1,0},{2,3},{3,2},{4,5},{5,4},{6,7},{7,6},{8,9},{9,8},{10,11... | collective-permute-start | bytes 3145736 | tf_op jit(solution)/shard_map/ppermute | solution.py:655
  220.2 11.0 %collective-permute-start.8 = (bf16[1024,2816]{1,0:T(8,128)(2,1)}, bf16[1024,2816]{1,0:T(8,128)(2,1)}, u32[]{:S(2)}, u32[]{:S(2)}) collective-permute-start(bf16[1024,2816]{1,0:T(8,128)(2,1)} %shard_map.498), channel_id=1, source_target_pairs={{0,2},{2,0},{4,6},{6,4},{8,10},{10,8},{12,14},{14,12},{16,18},{18,... | collective-permute-start | bytes 17301512 | tf_op jit(solution)/shard_map/ppermute | solution.py:628
  254.5 280.9 %reduce-scatter.4.cloned.1.call-start = ((), (), s32[]{:S(2)}) async-start(), calls=%async_computation.6 | async-start | bytes 4718592 | tf_op jit(solution)/shard_map/reduce_scatter | solution.py:623
  282.4 25.6 %collective-permute-start.10 = (bf16[256,2048]{1,0:T(8,128)(2,1)}, bf16[256,2048]{1,0:T(8,128)(2,1)S(1)}, u32[]{:S(2)}, u32[]{:S(2)}) collective-permute-start(bf16[256,2048]{1,0:T(8,128)(2,1)} %shard_map.505), channel_id=1, source_target_pairs={{0,1},{1,0},{2,3},{3,2},{4,5},{5,4},{6,7},{7,6},{8,9},{9,8},{10,11... | collective-permute-start | bytes 3145736 | tf_op jit(solution)/shard_map/ppermute | solution.py:655
  315.1 24.8 %collective-permute-start.11 = (bf16[256,2048]{1,0:T(8,128)(2,1)}, bf16[256,2048]{1,0:T(8,128)(2,1)S(1)}, u32[]{:S(2)}, u32[]{:S(2)}) collective-permute-start(bf16[256,2048]{1,0:T(8,128)(2,1)} %get-tuple-element.104), channel_id=1, source_target_pairs={{0,1},{1,0},{2,3},{3,2},{4,5},{5,4},{6,7},{7,6},{8,9},{9,8},{10,11... | collective-permute-start | bytes 3145736 | tf_op jit(solution)/shard_map/ppermute | solution.py:655
  330.9 69.9 %collective-permute-start.23 = (bf16[1024,5632]{1,0:T(8,128)(2,1)}, bf16[1024,5632]{1,0:T(8,128)(2,1)}, u32[]{:S(2)}, u32[]{:S(2)}) collective-permute-start(bf16[1024,5632]{1,0:T(8,128)(2,1)} %shard_map.517), channel_id=1, source_target_pairs={{0,2},{2,0},{4,6},{6,4},{8,10},{10,8},{12,14},{14,12},{16,18},{18,... | collective-permute-start | bytes 34603016 | tf_op jit(solution)/shard_map/ppermute | solution.py:628
  372.6 16.5 %collective-permute-start.18 = (bf16[1024,1280]{1,0:T(8,128)(2,1)}, bf16[1024,1280]{1,0:T(8,128)(2,1)}, u32[]{:S(2)}, u32[]{:S(2)}) collective-permute-start(bf16[1024,1280]{1,0:T(8,128)(2,1)} %shard_map.511), channel_id=1, source_target_pairs={{0,2},{2,0},{4,6},{6,4},{8,10},{10,8},{12,14},{14,12},{16,18},{18,... | collective-permute-start | bytes 7864328 | tf_op jit(solution)/shard_map/ppermute | solution.py:628
  400.6 174.5 %reduce-scatter.6.cloned.1.call-start = ((), (), s32[]{:S(2)}) async-start(), calls=%async_computation.7 | async-start | bytes 12976128 | tf_op jit(solution)/shard_map/reduce_scatter | solution.py:623
  422.9 25.7 %collective-permute-start.12 = (bf16[256,2048]{1,0:T(8,128)(2,1)}, bf16[256,2048]{1,0:T(8,128)(2,1)S(1)}, u32[]{:S(2)}, u32[]{:S(2)}) collective-permute-start(bf16[256,2048]{1,0:T(8,128)(2,1)} %shard_map.509), channel_id=1, source_target_pairs={{0,1},{1,0},{2,3},{3,2},{4,5},{5,4},{6,7},{7,6},{8,9},{9,8},{10,11... | collective-permute-start | bytes 3145736 | tf_op jit(solution)/shard_map/ppermute | solution.py:655
  450.9 10.4 %collective-permute-start.13 = (f32[2,2048]{1,0:T(2,128)S(1)}, f32[2,2048]{1,0:T(2,128)S(1)}, u32[]{:S(2)}, u32[]{:S(2)}) collective-permute-start(f32[2,2048]{1,0:T(2,128)S(1)} %pad_maximum_fusion.6), channel_id=1, source_target_pairs={{0,1},{1,0},{2,3},{3,2},{4,5},{5,4},{6,7},{7,6},{8,9},{9,8},{10,11... | collective-permute-start | bytes 49160 | tf_op jit(solution)/shard_map/ppermute | solution.py:655
  461.3 24.2 %collective-permute-start.9 = (bf16[256,2048]{1,0:T(8,128)(2,1)}, bf16[256,2048]{1,0:T(8,128)(2,1)}, u32[]{:S(2)}, u32[]{:S(2)}) collective-permute-start(bf16[256,2048]{1,0:T(8,128)(2,1)} %shard_map.501), channel_id=1, source_target_pairs={{0,1},{1,0},{2,3},{3,2},{4,5},{5,4},{6,7},{7,6},{8,9},{9,8},{10,11... | collective-permute-start | bytes 3145736 | tf_op jit(solution)/shard_map/ppermute | solution.py:655
  461.4 8.3 %collective-permute-start.14 = (f32[2,2048]{1,0:T(2,128)S(1)}, f32[2,2048]{1,0:T(2,128)S(1)}, u32[]{:S(2)}, u32[]{:S(2)}) collective-permute-start(f32[2,2048]{1,0:T(2,128)S(1)} %fusion.11), channel_id=1, source_target_pairs={{0,2},{2,0},{4,6},{6,4},{8,10},{10,8},{12,14},{14,12},{16,18},{18,... | collective-permute-start | bytes 49160 | tf_op jit(solution)/shard_map/ppermute | solution.py:757
  469.7 24.1 %collective-permute-start.15 = (f32[2,2048]{1,0:T(2,128)S(1)}, f32[2,2048]{1,0:T(2,128)S(1)}, u32[]{:S(2)}, u32[]{:S(2)}) collective-permute-start(f32[2,2048]{1,0:T(2,128)S(1)} %fusion.16), channel_id=1, source_target_pairs={{0,4},{2,6},{4,0},{6,2},{8,12},{10,14},{12,8},{14,10},{16,20},{18,... | collective-permute-start | bytes 49160 | tf_op jit(solution)/shard_map/ppermute | solution.py:757
  496.4 13.8 %collective-permute-start.20 = (bf16[4,128,256]{2,1,0:T(8,128)(2,1)S(1)}, bf16[4,128,256]{2,1,0:T(8,128)(2,1)S(1)}, u32[]{:S(2)}, u32[]{:S(2)}) collective-permute-start(bf16[4,128,256]{2,1,0:T(8,128)(2,1)S(1)} %bitcast.86), channel_id=1, source_target_pairs={{0,4},{8,12},{16,20},{24,28},{28,24},{20,16},{12,8},{4,0},{2,6},{1... | collective-permute-start | bytes 786440 | tf_op jit(solution)/shard_map/ppermute | solution.py:637
  498.0 19.1 %collective-permute-start.17 = (f32[2,2048]{1,0:T(2,128)S(1)}, f32[2,2048]{1,0:T(2,128)S(1)}, u32[]{:S(2)}, u32[]{:S(2)}) collective-permute-start(f32[2,2048]{1,0:T(2,128)S(1)} %add.151), channel_id=1, source_target_pairs={{0,16},{2,18},{4,20},{6,22},{8,24},{10,26},{12,28},{14,30},{16,0},... | collective-permute-start | bytes 49160 | tf_op jit(solution)/shard_map/ppermute | solution.py:757
  511.1 7.9 %collective-permute-start.21 = (bf16[2,128,256]{2,1,0:T(8,128)(2,1)S(1)}, bf16[2,128,256]{2,1,0:T(8,128)(2,1)S(1)}, u32[]{:S(2)}, u32[]{:S(2)}) collective-permute-start(bf16[2,128,256]{2,1,0:T(8,128)(2,1)S(1)} %fusion.3), channel_id=1, source_target_pairs={{0,8},{8,0},{16,24},{24,16},{28,20},{20,28},{12,4},{4,12},{2,10},{... | collective-permute-start | bytes 393224 | tf_op jit(solution)/shard_map/ppermute | solution.py:637
  519.1 7.4 %collective-permute-start.22 = (bf16[1,128,256]{2,1,0:T(8,128)(2,1)S(1)}, bf16[1,128,256]{2,1,0:T(8,128)(2,1)S(1)}, u32[]{:S(2)}, u32[]{:S(2)}) collective-permute-start(bf16[1,128,256]{2,1,0:T(8,128)(2,1)S(1)} %fusion.5), channel_id=1, source_target_pairs={{0,16},{8,24},{16,0},{24,8},{28,12},{20,4},{12,28},{4,20},{2,18},{... | collective-permute-start | bytes 196616 | tf_op jit(solution)/shard_map/ppermute | solution.py:637
  (26 other events, 165.8 us)
Sparse Core Ops, SparseCore 0:
  10.2 57.5 all-gather.3
  69.9 118.6 all-gather.5
  190.2 64.3 all-gather.7
  256.7 63.2 reduce-scatter.7
  400.7 48.4 reduce-scatter.3
  451.3 123.6 reduce-scatter.5
